TPU v7x, 256 devices: a whole 4x4x8 slice. The times are simulated.
256 devices in a mesh: grp: 8 (over z_hi, core), dev: 32 (over z_lo, y, x).
Axes of the slice: x: 4, y: 4, z: 8 (z_hi: 4, z_lo: 2; z = z_hi * 2 + z_lo), core: 2. Of those that a mesh axis runs over, the one named last changes fastest.
Arguments:
- user_factors: float32 [32768, 256], P(('grp', 'dev')), may hold values from -0.5 to 0.5
- item_factors: float32 [16384, 256], P(('grp', 'dev')), may hold values from -0.5 to 0.5
- user_items: int32 [32768, 8, 3], P(('grp', 'dev')), may hold values from 0 to 2047, as said below
- user_conf: float32 [32768, 8, 3], P(('grp', 'dev')), may hold values from 1 to 200
- user_mask: int32 [32768, 8, 3], P(('grp', 'dev')), may hold values 0 or 1
- item_users: int32 [16384, 8, 6], P(('grp', 'dev')), may hold values from 0 to 4095, as said below
- item_conf: float32 [16384, 8, 6], P(('grp', 'dev')), may hold values from 1 to 200
- item_mask: int32 [16384, 8, 6], P(('grp', 'dev')), may hold values 0 or 1
Outputs:
- new_users: float32 [32768, 256], P(('grp', 'dev'))
- new_items: float32 [16384, 256], P(('grp', 'dev'))
Inputs may be any that keep to these rules, and one draw needn't show every extreme that they name: Within owner block c, id // 64 is the owner device and id % 64 its row. The user_items of the users of one device, in one owner block, name at most 16 distinct rows of any one owner device, and in every block each device names exactly 16 distinct rows of some owner device. Within owner block c, id // 128 is the owner device and id % 128 its row. The item_users of the items of one device, in one owner block, name at most 16 distinct rows of any one owner device, and in every block each device names exactly 16 distinct rows of some owner device.
All inputs are finite; a program needn't handle non-finite values. No bound on the sum of `user_mask` or of `item_mask` on one device may be relied on, other than what follows from the above.
Results may differ from a plain program's by a relative error of at most 0.0044.
Values may be sent and summed in bfloat16 or wider, within the bound.
A program may use at most 128 MiB of HBM per device.

v0:
```python
import jax
import jax.numpy as jnp
from jax import lax
from jax.sharding import Mesh
from jax.sharding import PartitionSpec as P

CG_STEPS = 4
GRP = ("grp_0", "grp_1")
GRP_DEV = ("grp_0", "grp_1", "dev")


ridge = 1.0


def joined_along(blocks, dim):
    dims = list(blocks.shape[1:])
    dims[dim] *= blocks.shape[0]
    return jnp.moveaxis(blocks, 0, dim).reshape(dims)


def gather_in_order(array, axes, turns):
    blocks = array
    for k in turns:
        blocks = lax.all_gather(blocks, axes[k])
    done = turns[::-1]
    back = [done.index(k) for k in range(len(axes))]
    blocks = blocks.transpose(*back, *range(len(axes), blocks.ndim))
    return blocks.reshape(-1, *array.shape)


def whole_of(array, axes, turns, dim):
    return joined_along(gather_in_order(array, axes, turns), dim)


def solve_rows(gram, start_x, rows, confidence, slot_mask):
    maskf = slot_mask.astype(jnp.float32)
    weight = confidence * maskf
    rhs = jnp.einsum(
        "us,usr->ur", maskf * (1.0 + confidence), rows, precision=lax.Precision.HIGHEST
    )

    def apply(vector):
        along = jnp.einsum("usr,ur->us", rows, vector, precision=lax.Precision.HIGHEST)
        extra = jnp.einsum("us,usr->ur", weight * along, rows, precision=lax.Precision.HIGHEST)
        return jnp.dot(vector, gram, precision=lax.Precision.HIGHEST) + ridge * vector + extra

    solution = start_x
    resid = rhs - apply(solution)
    direction = resid
    norm_now = jnp.sum(resid * resid, axis=1, keepdims=True)
    for step in range(CG_STEPS):
        image = apply(direction)
        alpha = norm_now / jnp.sum(direction * image, axis=1, keepdims=True)
        solution = solution + alpha * direction
        resid = resid - alpha * image
        norm_next = jnp.sum(resid * resid, axis=1, keepdims=True)
        direction = resid + norm_next / norm_now * direction
        norm_now = norm_next
    return solution


def gram_of(block):
    return lax.dot_general(
        block, block, (((0,), (0,)), ((), ())), preferred_element_type=jnp.float32
    )


def collect(whole, row_index, mask_now):
    picked = jnp.take(whole, row_index, axis=0).astype(jnp.float32)
    return picked * mask_now[..., None].astype(jnp.float32)


def half_step(start_x, other, slot_ids, confidence, slot_mask):
    local_rows = other.shape[0]
    groups = lax.axis_size(GRP)
    packed = other.astype(jnp.bfloat16)
    row_parts = []
    conf_parts = []
    mask_parts = []
    stacked = whole_of(packed, GRP, (0, 1), 0)
    whole = lax.all_gather(stacked, "dev", axis=0, tiled=True)
    for span in range(groups):
        local = slot_ids[:, span, :]
        row_index = (
            local // local_rows * (groups * local_rows) + span * local_rows + local % local_rows
        )
        row_parts.append(collect(whole, row_index, slot_mask[:, span, :]))
        conf_parts.append(confidence[:, span, :])
        mask_parts.append(slot_mask[:, span, :])
    squares = gram_of(whole)
    rows = jnp.concatenate(row_parts, axis=1)
    conf_all = jnp.concatenate(conf_parts, axis=1)
    mask_all = jnp.concatenate(mask_parts, axis=1)
    return solve_rows(squares, start_x, rows, conf_all, mask_all)


def per_device(
    user_factors, item_factors, user_items, user_conf, user_mask, item_users, item_conf, item_mask
):
    new_users = half_step(user_factors, item_factors, user_items, user_conf, user_mask)
    new_items = half_step(item_factors, new_users, item_users, item_conf, item_mask)
    return (new_users, new_items)


def solution(mesh):
    finer = Mesh(mesh.devices.reshape(4, 2, mesh.shape["dev"]), ("grp_0", "grp_1", "dev"))
    in_specs = (
        P(GRP_DEV, None),
        P(GRP_DEV, None),
        P(GRP_DEV, None, None),
        P(GRP_DEV, None, None),
        P(GRP_DEV, None, None),
        P(GRP_DEV, None, None),
        P(GRP_DEV, None, None),
        P(GRP_DEV, None, None),
    )
    out_specs = (P(GRP_DEV, None), P(GRP_DEV, None))
    return jax.shard_map(
        per_device, mesh=finer, in_specs=in_specs, out_specs=out_specs, check_vma=False
    )
```

profile of v0, /device:TPU:1, one launch (start us, length us, event | category | flops | bytes accessed | tf_op | source)
XLA Modules:
  0.0 744.5 jit_solution(14757438769674752799)
XLA Ops:
  8.1 15.5 %all-gather = bf16[256,256]{1,0:T(8,128)(2,1)S(1)} all-gather(bf16[64,256]{1,0:T(8,128)(2,1)S(1)} %convert_element_type.189), channel_id=2, replica_groups=mesh['grp_0'=4,'grp_1'=2,'dev'=32] {'grp_0'}, dimensions={0}, use_global_device_ids=true | all-gather | bytes 163840 | tf_op jit(solution)/shard_map/all_gather | solution.py:24
  38.0 139.0 %all-gather.7.cloned.1.call-done = bf16[16384,256]{1,0:T(8,128)(2,1)} async-done(((bf16[512,256]{1,0:T(8,128)(2,1)}), bf16[16384,256]{1,0:T(8,128)(2,1)}) %all-gather.7.cloned.1.call-update) | async-done | bytes 8388624 | tf_op jit(solution)/shard_map/all_gather | solution.py:81
  183.2 6.1 gather_fusion.6
  189.5 6.1 gather_fusion.5
  195.7 6.1 gather_fusion.4
  202.0 6.1 gather_fusion.3
  208.2 6.7 gather_fusion.2
  215.0 6.1 gather_fusion.1
  221.2 6.1 gather_fusion
  236.6 22.3 %concatenate.20 = f32[128,24,256]{2,1,0:T(8,128)S(1)} concatenate(f32[128,3,256]{2,1,0:T(4,128)} %convert_multiply_fusion.15, f32[128,3,256]{2,1,0:T(4,128)} %convert_multiply_fusion.14, f32[128,3,256]{2,1,0:T(4,128)} %convert_multiply_fusion.13, f32[128,3,256]{2,1,0:T(4,128)} %convert_multiply_fusion.12, f32[128,3,256]{2,1,0:T(4,128)} %convert_multiply_fusion.11, ...), dimensions={1} | concatenate | bytes 6291456 | tf_op jit(solution)/shard_map/concatenate | solution.py:91
  264.8 8.2 %fusion.190 = f32[256,256]{1,0:T(8,128)S(1)} fusion(bf16[16384,256]{1,0:T(8,128)(2,1)} %all-gather.7.cloned.1.call-done), kind=kOutput, calls=%fused_computation.457 | convolution fusion | flops 2147483648 | bytes 8650752 | tf_op jit(solution)/shard_map/dot_general | solution.py:63
  337.5 13.1 %all-gather.2 = bf16[512,256]{0,1:T(8,128)(2,1)S(1)} all-gather(bf16[128,256]{0,1:T(8,128)(2,1)S(1)} %get-tuple-element.36), channel_id=4, replica_groups=mesh['grp_0'=4,'grp_1'=2,'dev'=32] {'grp_0'}, dimensions={0}, use_global_device_ids=true | all-gather | bytes 327680 | tf_op jit(solution)/shard_map/all_gather | solution.py:24
  350.7 25.6 %all-gather.3 = bf16[8,128,256]{2,1,0:T(8,128)(2,1)S(1)} all-gather(bf16[4,128,256]{2,1,0:T(8,128)(2,1)S(1)} %bitcast.642), channel_id=5, replica_groups=mesh['grp_0'=4,'grp_1'=2,'dev'=32] {'grp_1'}, dimensions={0}, use_global_device_ids=true | all-gather | bytes 786432 | tf_op jit(solution)/shard_map/all_gather | solution.py:24
  383.0 185.0 %all-gather.9.cloned.1.call-done = bf16[32768,256]{1,0:T(8,128)(2,1)} async-done(((bf16[1024,256]{1,0:T(8,128)(2,1)}), bf16[32768,256]{1,0:T(8,128)(2,1)}) %all-gather.9.cloned.1.call-update) | async-done | bytes 16777232 | tf_op jit(solution)/shard_map/all_gather | solution.py:81
  568.0 9.6 %gather_fusion.15 = bf16[384,256]{1,0:T(8,128)(2,1)S(1)} fusion(bf16[32768,256]{1,0:T(8,128)(2,1)} %all-gather.9.cloned.1.call-done, s32[1024]{0:T(1024)S(1)} %pad_clamp_fusion), kind=kCustom, calls=%fused_computation.15.clone | custom fusion | bytes 394752 | tf_op jit(solution)/shard_map/jit(_take)/gather | solution.py:69
  577.7 9.6 %gather_fusion.14 = bf16[384,256]{1,0:T(8,128)(2,1)S(1)} fusion(bf16[32768,256]{1,0:T(8,128)(2,1)} %all-gather.9.cloned.1.call-done, s32[1024]{0:T(1024)S(1)} %pad_clamp_fusion.1), kind=kCustom, calls=%fused_computation.14.clone | custom fusion | bytes 394752 | tf_op jit(solution)/shard_map/jit(_take)/gather | solution.py:69
  587.4 9.6 %gather_fusion.13 = bf16[384,256]{1,0:T(8,128)(2,1)S(1)} fusion(bf16[32768,256]{1,0:T(8,128)(2,1)} %all-gather.9.cloned.1.call-done, s32[1024]{0:T(1024)S(1)} %pad_clamp_fusion.2), kind=kCustom, calls=%fused_computation.13.clone | custom fusion | bytes 394752 | tf_op jit(solution)/shard_map/jit(_take)/gather | solution.py:69
  597.0 9.8 %gather_fusion.12 = bf16[384,256]{1,0:T(8,128)(2,1)S(1)} fusion(bf16[32768,256]{1,0:T(8,128)(2,1)} %all-gather.9.cloned.1.call-done, s32[1024]{0:T(1024)S(1)} %pad_clamp_fusion.3), kind=kCustom, calls=%fused_computation.12.clone | custom fusion | bytes 394752 | tf_op jit(solution)/shard_map/jit(_take)/gather | solution.py:69
  606.9 9.6 %gather_fusion.11 = bf16[384,256]{1,0:T(8,128)(2,1)S(1)} fusion(bf16[32768,256]{1,0:T(8,128)(2,1)} %all-gather.9.cloned.1.call-done, s32[1024]{0:T(1024)S(1)} %pad_clamp_fusion.4), kind=kCustom, calls=%fused_computation.11.clone | custom fusion | bytes 394752 | tf_op jit(solution)/shard_map/jit(_take)/gather | solution.py:69
  616.6 9.6 %gather_fusion.10 = bf16[384,256]{1,0:T(8,128)(2,1)S(1)} fusion(bf16[32768,256]{1,0:T(8,128)(2,1)} %all-gather.9.cloned.1.call-done, s32[1024]{0:T(1024)S(1)} %pad_clamp_fusion.5), kind=kCustom, calls=%fused_computation.10.clone | custom fusion | bytes 394752 | tf_op jit(solution)/shard_map/jit(_take)/gather | solution.py:69
  626.3 9.6 %gather_fusion.9 = bf16[384,256]{1,0:T(8,128)(2,1)S(1)} fusion(bf16[32768,256]{1,0:T(8,128)(2,1)} %all-gather.9.cloned.1.call-done, s32[1024]{0:T(1024)S(1)} %pad_clamp_fusion.6), kind=kCustom, calls=%fused_computation.9.clone | custom fusion | bytes 394752 | tf_op jit(solution)/shard_map/jit(_take)/gather | solution.py:69
  635.9 9.8 %gather_fusion.8 = bf16[384,256]{1,0:T(8,128)(2,1)S(1)} fusion(bf16[32768,256]{1,0:T(8,128)(2,1)} %all-gather.9.cloned.1.call-done, s32[1024]{0:T(1024)S(1)} %pad_clamp_fusion.7), kind=kCustom, calls=%fused_computation.1.clone | custom fusion | bytes 394752 | tf_op jit(solution)/shard_map/jit(_take)/gather | solution.py:69
  653.8 20.6 %concatenate.23 = f32[64,48,256]{2,1,0:T(8,128)S(1)} concatenate(f32[64,6,256]{2,1,0:T(8,128)} %convert_multiply_fusion.7, f32[64,6,256]{2,1,0:T(8,128)} %convert_multiply_fusion.6, f32[64,6,256]{2,1,0:T(8,128)} %convert_multiply_fusion.5, f32[64,6,256]{2,1,0:T(8,128)} %convert_multiply_fusion.4, f32[64,6,256]{2,1,0:T(8,128)} %convert_multiply_fusion.3, ...), dimensions={1} | concatenate | bytes 6291456 | tf_op jit(solution)/shard_map/concatenate | solution.py:91
  682.0 14.5 %fusion.192 = f32[256,256]{1,0:T(8,128)S(1)} fusion(bf16[32768,256]{1,0:T(8,128)(2,1)} %all-gather.9.cloned.1.call-done), kind=kOutput, calls=%fused_computation.459 | convolution fusion | flops 4294967296 | bytes 17039360 | tf_op jit(solution)/shard_map/dot_general | solution.py:63
  (321 shorter events, 165.0 us)
Async XLA Ops:
  7.2 29.2 %copy-start.5 = (f32[128,256]{1,0:T(8,128)S(1)}, f32[128,256]{1,0:T(8,128)}, u32[]{:S(2)}) copy-start(f32[128,256]{1,0:T(8,128)} %param.12) | copy-start | bytes 393220
  7.2 29.9 %copy-start.23 = (f32[128,8,3]{0,1,2:T(8,128)S(1)}, f32[128,8,3]{0,1,2:T(8,128)}, u32[]{:S(2)}) copy-start(f32[128,8,3]{0,1,2:T(8,128)} %param.15) | copy-start | bytes 36868
  7.2 169.8 %all-gather.7.cloned.1.call-start = ((), (), s32[]{:S(2)}) async-start(), calls=%async_computation | async-start | bytes 8650752 | tf_op jit(solution)/shard_map/all_gather | solution.py:81
  29.4 538.6 %all-gather.9.cloned.1.call-start = ((), (), s32[]{:S(2)}) async-start(), calls=%async_computation.1 | async-start | bytes 17301504 | tf_op jit(solution)/shard_map/all_gather | solution.py:81
  264.8 8.2 %copy-start.6 = (f32[128,256]{1,0:T(8,128)S(1)}, f32[128,256]{1,0:T(8,128)}, u32[]{:S(2)}) copy-start(f32[128,256]{1,0:T(8,128)} %param.12) | copy-start | bytes 393220
  264.8 8.2 %copy-start.7 = (f32[128,256]{0,1:T(8,128)S(1)}, f32[128,256]{0,1:T(8,128)}, u32[]{:S(2)}) copy-start(f32[128,256]{0,1:T(8,128)} %copy.246) | copy-start | bytes 393220
  264.8 8.2 %copy-start.17 = (f32[128,256]{0,1:T(8,128)S(1)}, f32[128,256]{0,1:T(8,128)}, u32[]{:S(2)}) copy-start(f32[128,256]{0,1:T(8,128)} %copy.310) | copy-start | bytes 393220
  264.8 8.2 %copy-start.18 = (f32[128,256]{0,1:T(8,128)S(1)}, f32[128,256]{0,1:T(8,128)}, u32[]{:S(2)}) copy-start(f32[128,256]{0,1:T(8,128)} %copy.304) | copy-start | bytes 393220
  301.4 1.0 copy-start.25
  302.4 1.2 copy-start.1
  319.2 2.1 copy-start.24
  333.1 44.0 %copy-start.20 = (s32[64,8,6]{0,1,2:T(8,128)S(1)}, s32[64,8,6]{0,1,2:T(8,128)}, u32[]{:S(2)}) copy-start(s32[64,8,6]{0,1,2:T(8,128)} %param.17) | copy-start | bytes 36868
  333.1 45.1 %copy-start.21 = (s32[64,8,6]{0,1,2:T(8,128)S(1)}, s32[64,8,6]{0,1,2:T(8,128)}, u32[]{:S(2)}) copy-start(s32[64,8,6]{0,1,2:T(8,128)} %param.19) | copy-start | bytes 36868
  333.1 47.8 %copy-start.22 = (f32[64,8,6]{0,1,2:T(8,128)S(1)}, f32[64,8,6]{0,1,2:T(8,128)}, u32[]{:S(2)}) copy-start(f32[64,8,6]{0,1,2:T(8,128)} %param.18) | copy-start | bytes 36868
  653.8 20.6 %copy-start.14 = (f32[64,256]{1,0:T(8,128)S(1)}, f32[64,256]{1,0:T(8,128)}, u32[]{:S(2)}) copy-start(f32[64,256]{1,0:T(8,128)} %param.13) | copy-start | bytes 196612
  682.0 14.5 %copy-start.19 = (f32[64,1,256]{2,1,0:T(1,128)S(1)}, f32[64,1,256]{2,1,0:T(1,128)}, u32[]{:S(2)}) copy-start(f32[64,1,256]{2,1,0:T(1,128)} %fusion.193) | copy-start | bytes 196612
  696.8 2.8 copy-start.16
  710.0 2.8 copy-start.9
  722.0 2.6 copy-start.3
  722.0 3.0 copy-start.11
  726.3 10.4 %copy-start.30 = (f32[64]{0:T(128)S(1)}, f32[64]{0:T(128)}, u32[]{:S(2)}) copy-start(f32[64]{0:T(128)} %copy-done.29) | copy-start | bytes 772
  733.9 2.4 copy-start.13
  733.9 2.8 copy-start.4
  733.9 2.8 copy-start.15
  (9 other events, 5.4 us)
Sparse Core Ops, SparseCore 0:
  29.5 147.4 all-gather.6
  377.2 190.7 all-gather.8
where the time goes:
time: 751 us; the launch traced here: 745 us
  waiting for transfers between devices  324 us (43%)
  local copies, waits for them, and re-layouts  225 us (30%)
  matrix products  62.8 us (8%)
  blocking collectives  59.2 us (8%)
  other arithmetic  58.1 us (8%)
  between operations  15.2 us (2%)
    all_gather x2, waiting for transfers between devices, half_step(): whole = lax.all_gather(stacked, 'dev', axis=0, tiled=True)  324 us
    gather x32, local copies, waits for them, and re-layouts, collect(): picked = jnp.take(whole, row_index, axis=0).astype(jnp.float32)  128 us
    all_gather x4, blocking collectives, gather_in_order(): blocks = lax.all_gather(blocks, axes[k])  59.2 us
    concatenate x2, local copies, waits for them, and re-layouts, half_step(): rows = jnp.concatenate(row_parts, axis=1)  42.9 us
    dot_general x2, matrix products, gram_of(): lax.dot_general(block, block, (((0,), (0,)), ((), ())), preferred_element...  22.7 us
    dot_general x6, matrix products, apply(): jnp.einsum('usr,ur->us', rows, vector, precision=lax.Precision.HIGHEST)  18.5 us
    unnamed x9, other arithmetic  18 us
    unnamed x74, local copies, waits for them, and re-layouts  17.6 us
  transfers between devices with their start and end apart: 2, of which 2 were waited for; matrix products, arithmetic and copies ran while one was open for 2% of the time, Pallas kernels for 0%

commit v1 on v0

v1 whole, which is shorter than its diff:
```python
import functools

import jax
import jax.numpy as jnp
from jax import lax
from jax.experimental import pallas as pl
from jax.experimental.pallas import tpu as pltpu
from jax.sharding import PartitionSpec as P

MESH = pl.DeviceIdType.MESH
CG_STEPS = 4
RANK = 256
NX, NY, NZ = 4, 4, 8
SIZES = {"x": NX, "y": NY, "z": NZ}
ORDERS = (("z", "y", "x"), ("z", "x", "y"), ("x", "y", "z"))


def units_of(rows):
    units = rows // 16 * 2
    last = units // 4
    side = (units - last) // 2
    return (side, side, last)


def buffer_shape(order, units):
    return (2,) + tuple(SIZES[a] for a in order[::-1]) + (units, 16, 128)


def my_coords():
    grp, dev = lax.axis_index("grp"), lax.axis_index("dev")
    core = grp % 2
    z = grp // 2 * 2 + dev // 16
    return {"core": core, "z": z, "y": dev // 4 % 4, "x": dev % 4}


def device_at(coords):
    return {
        "grp": coords["z"] // 2 * 2 + coords["core"],
        "dev": coords["z"] % 2 * 16 + coords["y"] * 4 + coords["x"],
    }


def neighbour(me, axis, shift):
    there = dict(me)
    size = SIZES[axis]
    there[axis] = (me[axis] + shift + size) % size
    return device_at(there)


def gather_kernel(*refs):
    ins, outs = refs[:3], refs[3:6]
    send_sem, recv_sem, local_sem = refs[6:]
    me = my_coords()
    core = me["core"]
    partner = device_at({**me, "core": 1 - core})

    barrier = pltpu.get_barrier_semaphore()
    around = [partner] + [neighbour(me, a, s) for a in "xyz" for s in (1, -1)]
    for other in around:
        pl.semaphore_signal(barrier, inc=1, device_id=other, device_id_type=MESH)
    pl.semaphore_wait(barrier, len(around))

    issued = []
    hand_overs = []
    counter = [0]

    def remote(src, dst, target):
        e = counter[0]
        counter[0] += 1
        copy = pltpu.make_async_remote_copy(
            src_ref=src,
            dst_ref=dst,
            send_sem=send_sem.at[e],
            recv_sem=recv_sem.at[e],
            device_id=target,
            device_id_type=MESH,
        )
        copy.start()
        issued.append(copy)
        return copy

    def block(colour, phase, v, half=None):
        order = ORDERS[colour]
        ref = outs[colour]
        index = [core] + [me[order[k]] for k in range(2, phase, -1)] + [v]
        if half is not None:
            inner = ref.shape[len(index)]
            cut = inner // 2
            index.append(pl.ds(0, cut) if half == 0 else pl.ds(cut, inner - cut))
        return ref.at[tuple(index)]

    steps = []
    for colour, order in enumerate(ORDERS):
        steps.append([(ph, k) for ph in range(3) for k in range(SIZES[order[ph]] // 2)])
    local = []
    for colour in range(3):
        own = outs[colour].at[(core,) + tuple(me[a] for a in ORDERS[colour][::-1])]
        copy = pltpu.make_async_copy(ins[colour], own, local_sem.at[colour])
        copy.start()
        local.append(copy)

    flying = [None] * 3

    def send(colour, phase, k):
        axis = ORDERS[colour][phase]
        size = SIZES[axis]
        last = k == size // 2 - 1
        pair = []
        for way in (0, 1):
            shift = 1 if way == 0 else -1
            v = (me[axis] - shift * k + size) % size
            half = way if last and size > 2 else None
            dst = block(colour, phase, v, half)
            src = dst
            if phase == 0 and k == 0:
                src = ins[colour]
            pair.append(remote(src, dst, neighbour(me, axis, shift)))
        flying[colour] = (phase, k, pair)

    def arrived(colour, way):
        phase, k, pair = flying[colour]
        pair[way].wait_recv()
        if phase == 2:
            axis = ORDERS[colour][phase]
            size = SIZES[axis]
            shift = 1 if way == 0 else -1
            v = (me[axis] - shift * (k + 1) + 2 * size) % size
            half = way if k == size // 2 - 1 else None
            got = block(colour, phase, v, half)
            hand_overs.append(remote(got, got, partner))

    for r in range(max(len(s) for s in steps) + 1):
        for colour in range(3):
            if r > len(steps[colour]):
                continue
            if r > 0:
                for way in (0, 1):
                    arrived(colour, way)
            if r == len(steps[colour]):
                continue
            phase, k = steps[colour][r]
            if phase == 1 and k == 0:
                local[colour].wait()
            if phase == 2 and k == 0:
                slab = block(colour, 2, me[ORDERS[colour][2]])
                hand_overs.append(remote(slab, slab, partner))
            send(colour, phase, k)
    for copy in hand_overs:
        copy.wait_recv()
    for copy in issued:
        copy.wait_send()


def copies_of():
    total = 0
    for order in ORDERS:
        total += 2 * sum(SIZES[a] // 2 for a in order)
        total += 1 + 2 * (SIZES[order[2]] // 2)
    return total


def gather_table(pieces, collective_id):
    copies = copies_of()
    units = [p.shape[0] for p in pieces]
    return pl.pallas_call(
        gather_kernel,
        out_shape=[
            jax.ShapeDtypeStruct(buffer_shape(o, u), jnp.bfloat16) for o, u in zip(ORDERS, units)
        ],
        in_specs=[pl.BlockSpec(memory_space=pltpu.VMEM)] * 3,
        out_specs=[pl.BlockSpec(memory_space=pl.ANY)] * 3,
        scratch_shapes=[
            pltpu.SemaphoreType.DMA((copies,)),
            pltpu.SemaphoreType.DMA((copies,)),
            pltpu.SemaphoreType.DMA((3,)),
        ],
        compiler_params=pltpu.CompilerParams(collective_id=collective_id, has_side_effects=True),
        name=f"gather_table_{collective_id}",
    )(*pieces)


def split_two(value):
    high = value.astype(jnp.bfloat16)
    low = (value - high.astype(jnp.float32)).astype(jnp.bfloat16)
    return jnp.concatenate([high, low], axis=0)


def dot(a, b):
    return jnp.dot(a, b, preferred_element_type=jnp.float32)


def solve_kernel(n, owner_rows, units, pack, *refs):
    tables = refs[:3]
    code_ref, weight_ref, gain_ref, start_ref = refs[3:7]
    out_ref = refs[7]
    packed = refs[8:11] if pack else ()
    scratch = refs[8 + len(packed):]
    (both, flipped, picked_t, picked, gram, gram2, diag, x_s, r_s, p_s) = scratch
    g = pl.program_id(0)
    slots = code_ref.shape[1]
    groups = owner_rows // 16
    total = slots * 8

    def tile(zl, y, x, j):
        if j < units[0]:
            return tables[0][0, x, y, zl, j]
        j -= units[0]
        if j < units[1]:
            return tables[1][0, y, x, zl, j]
        return tables[2][0, zl, y, x, j - units[1]]

    code = code_ref[pl.ds(g, 1), :]
    for chunk in range(2 * groups):
        zl, group = divmod(chunk, groups)
        span = pl.ds(chunk * 256, 256)
        halves = []
        for h in (0, 1):
            parts = [tile(zl, y, x, 2 * group + h) for y in range(NY) for x in range(NX)]
            halves.append(jnp.concatenate(parts, axis=0))
        rows = jnp.concatenate(halves, axis=1)
        both[span, 0:256] = rows
        flipped[:, span] = rows.T
        position = lax.broadcasted_iota(jnp.int32, (256, slots), 0) + chunk * 256
        both[span, 256 : 256 + slots] = jnp.where(position == code, 1.0, 0.0).astype(jnp.bfloat16)
    product = dot(flipped[...], both[...])

    @pl.when(g == 0)
    def _():
        gram[...] = product[:, 0:256]

    @pl.when(g > 0)
    def _():
        gram[...] += product[:, 0:256]

    here = product[:, 256 : 256 + slots]
    lanes = pl.ds(pl.multiple_of(g * slots, 128), slots)
    picked_t[:, lanes] = here.astype(jnp.bfloat16)
    picked[pl.ds(pl.multiple_of(g * slots, 128), slots), :] = here.T.astype(jnp.bfloat16)
    lane = lax.broadcasted_iota(jnp.int32, (n, slots), 1)
    own = lane % n == lax.broadcasted_iota(jnp.int32, (n, slots), 0)
    diag[:, lanes] = jnp.where(own, weight_ref[pl.ds(g, 1), :], 0.0)

    @pl.when(g == 7)
    def _():
        whole = gram[...]
        high = whole.astype(jnp.bfloat16)
        gram2[:, 0:256] = high
        gram2[:, 256:512] = (whole - high.astype(jnp.float32)).astype(jnp.bfloat16)
        width = 768

        def apply(vector):
            two = split_two(vector)
            by_gram = dot(two, gram2[...])
            image = by_gram[:n, :256] + by_gram[:n, 256:] + by_gram[n:, :256] + vector
            extra = jnp.zeros((2 * n, RANK), jnp.float32)
            for at in range(0, total, width):
                along = dot(two, picked_t[:, at : at + width])
                along = (along[:n] + along[n:]) * diag[:, at : at + width]
                extra = extra + dot(split_two(along), picked[at : at + width, :])
            return image + extra[:n] + extra[n:]

        rhs = jnp.zeros((2 * n, RANK), jnp.float32)
        for block in range(8):
            gains = jnp.where(own, gain_ref[block : block + 1, :], 0.0)
            rhs = rhs + dot(split_two(gains), picked[block * slots : (block + 1) * slots, :])
        start = start_ref[...]
        resid = rhs[:n] + rhs[n:] - apply(start)
        x_s[...] = start
        r_s[...] = resid
        p_s[...] = resid

        def step(_, now):
            direction = p_s[...]
            image = apply(direction)
            alpha = now / jnp.sum(direction * image, axis=1, keepdims=True)
            x_s[...] += alpha * direction
            left = r_s[...] - alpha * image
            r_s[...] = left
            later = jnp.sum(left * left, axis=1, keepdims=True)
            p_s[...] = left + later / now * direction
            return later

        lax.fori_loop(0, CG_STEPS, step, jnp.sum(resid * resid, axis=1, keepdims=True))
        out = x_s[...]
        out_ref[...] = out
        if pack:
            small = out.astype(jnp.bfloat16)
            many = units_of(n)
            for j in range(n // 8):
                piece = small[j // 2 * 16 : j // 2 * 16 + 16, j % 2 * 128 : j % 2 * 128 + 128]
                if j < many[0]:
                    packed[0][j] = piece
                elif j < many[0] + many[1]:
                    packed[1][j - many[0]] = piece
                else:
                    packed[2][j - many[0] - many[1]] = piece


def solve(tables, codes, weights, gains, start, owner_rows, pack):
    n = start.shape[0]
    units = [t.shape[4] for t in tables]
    slots = codes.shape[1]
    depth = 2 * 16 * owner_rows
    whole = lambda shape: pl.BlockSpec(shape, lambda g: (0,) * len(shape))
    table_specs = [
        pl.BlockSpec((1, 4, 4, 2, units[0], 16, 128), lambda g: (g % 2, 0, 0, g // 2, 0, 0, 0)),
        pl.BlockSpec((1, 4, 4, 2, units[1], 16, 128), lambda g: (g % 2, 0, 0, g // 2, 0, 0, 0)),
        pl.BlockSpec((1, 2, 4, 4, units[2], 16, 128), lambda g: (g % 2, g // 2, 0, 0, 0, 0, 0)),
    ]
    out_shape = [jax.ShapeDtypeStruct((n, RANK), jnp.float32)]
    if pack:
        out_shape += [jax.ShapeDtypeStruct((u, 16, 128), jnp.bfloat16) for u in units_of(n)]
    return pl.pallas_call(
        functools.partial(solve_kernel, n, owner_rows, units, pack),
        grid=(8,),
        out_shape=out_shape,
        in_specs=table_specs + [whole(codes.shape)] * 3 + [whole(start.shape)],
        out_specs=[whole(s.shape) for s in out_shape],
        scratch_shapes=[
            pltpu.VMEM((depth, RANK + slots), jnp.bfloat16),
            pltpu.VMEM((RANK, depth), jnp.bfloat16),
            pltpu.VMEM((RANK, 8 * slots), jnp.bfloat16),
            pltpu.VMEM((8 * slots, RANK), jnp.bfloat16),
            pltpu.VMEM((RANK, RANK), jnp.float32),
            pltpu.VMEM((RANK, 2 * RANK), jnp.bfloat16),
            pltpu.VMEM((n, 8 * slots), jnp.float32),
            pltpu.VMEM((n, RANK), jnp.float32),
            pltpu.VMEM((n, RANK), jnp.float32),
            pltpu.VMEM((n, RANK), jnp.float32),
        ],
        compiler_params=pltpu.CompilerParams(
            dimension_semantics=("arbitrary",), vmem_limit_bytes=48 << 20
        ),
        name=f"solve_{n}",
    )(*tables, codes, weights, gains, start)


def slot_rows(array):
    n, blocks, slots = array.shape
    return array.transpose(1, 2, 0).reshape(blocks, slots * n)


def slot_inputs(slot_ids, confidence, slot_mask, owner_rows):
    ids = slot_rows(slot_ids)
    owner, row = ids // owner_rows, ids % owner_rows
    chunk = owner // 16 * (owner_rows // 16) + row // 16
    codes = chunk * 256 + owner % 16 * 16 + row % 16
    mask = slot_rows(slot_mask).astype(jnp.float32)
    conf = slot_rows(confidence)
    return codes, mask * conf, mask * (1.0 + conf)


def per_device(
    user_factors, item_factors, user_items, user_conf, user_mask, item_users, item_conf, item_mask
):
    users, items = user_factors.shape[0], item_factors.shape[0]
    small = item_factors.astype(jnp.bfloat16).reshape(items // 16, 16, 2, 128)
    small = small.transpose(0, 2, 1, 3).reshape(items // 8, 16, 128)
    counts = units_of(items)
    pieces = jnp.split(small, [counts[0], counts[0] + counts[1]])
    tables = gather_table(pieces, 0)
    solved = solve(tables, *slot_inputs(user_items, user_conf, user_mask, items), user_factors, items, True)
    new_users, pieces = solved[0], solved[1:]
    tables = gather_table(pieces, 1)
    new_items = solve(
        tables, *slot_inputs(item_users, item_conf, item_mask, users), item_factors, users, False
    )[0]
    return new_users, new_items


def solution(mesh):
    both = ("grp", "dev")
    two, three = P(both, None), P(both, None, None)
    return jax.shard_map(
        per_device,
        mesh=mesh,
        in_specs=(two, two) + (three,) * 6,
        out_specs=(two, two),
        check_vma=False,
    )
```

time: 751 us -> 170 us (0.23)
  waiting for transfers between devices: 324 us -> 0 us
  local copies, waits for them, and re-layouts: 225 us -> 9.85 us
  Pallas kernels: 0 us -> 156 us
  matrix products: 62.8 us -> 0 us
  blocking collectives: 59.2 us -> 0 us
  other arithmetic: 58.1 us -> 2.38 us
  between operations: 15.2 us -> 0.71 us
    all_gather x2 -> x0, waiting for transfers between devices: 324 us -> none  [half_step(): whole = lax.all_gather(stacked, 'dev', axis=0, tiled=True)]
    pallas_call x0 -> x4, Pallas kernels: none -> 156 us  [the longest x2 113 us: gather_table(): pl.pallas_call(gather_kernel, out_shape=[jax.ShapeDtypeStruct(buffer_shap...]
    gather x32 -> x0, local copies, waits for them, and re-layouts: 128 us -> none  [collect(): picked = jnp.take(whole, row_index, axis=0).astype(jnp.float32)]
    dot_general x24 -> x0, matrix products: 62.8 us -> none  [the longest x2 22.7 us: gram_of(): lax.dot_general(block, block, (((0,), (0,)), ((), ())), preferred_element...]
    all_gather x4 -> x0, blocking collectives: 59.2 us -> none  [gather_in_order(): blocks = lax.all_gather(blocks, axes[k])]
    concatenate x6 -> x0, local copies, waits for them, and re-layouts: 44.8 us -> none  [the longest x2 42.9 us: half_step(): rows = jnp.concatenate(row_parts, axis=1)]
    mul x26 -> x2, other arithmetic: 27.1 us -> 0.74 us  [slot_inputs(): return (codes, mask * conf, mask * (1.0 + conf))]
    unnamed x9 -> x0, other arithmetic: 18 us -> none
  transfers between devices with their start and end apart: 2 -> 0, of which waited for: 2 -> 0; matrix products, arithmetic and copies ran while one was open for 2% -> 0% of each run, Pallas kernels for 0% -> 0%
where the time goes in v1:
time: 170 us; the launch traced here: 169 us
  Pallas kernels  156 us (92%)
  local copies, waits for them, and re-layouts  9.85 us (6%)
  other arithmetic  2.38 us (1%)
    pallas_call x2, Pallas kernels, gather_table(): pl.pallas_call(gather_kernel, out_shape=[jax.ShapeDtypeStruct(buffer_shap...  113 us
    pallas_call x2, Pallas kernels, solve(): pl.pallas_call(functools.partial(solve_kernel, n, owner_rows, units, pack...  43.9 us
    unnamed x22, local copies, waits for them, and re-layouts  8.39 us

profile of v1, /device:TPU:1, one launch (start us, length us, event | category | flops | bytes accessed | tf_op | source)
XLA Modules:
  0.0 169.4 jit_solution(7999740810611265011)
XLA Ops:
  0.6 0.8 convert_element_type.21
  1.5 0.6 fusion.34
  2.1 0.6 slice_bitcast_fusion.refs_2_
  2.7 52.3 %gather_table_0.1 = (bf16[2,4,4,8,3,16,128]{6,5,4,3,2,1,0:T(8,128)(2,1)}, bf16[2,4,4,8,3,16,128]{6,5,4,3,2,1,0:T(8,128)(2,1)}, bf16[2,8,4,4,2,16,128]{6,5,4,3,2,1,0:T(8,128)(2,1)}) custom-call(bf16[3,16,128]{2,1,0:T(8,128)(2,1)} %get-tuple-element.25.refs_0_, bf16[3,16,128]{2,1,0:T(8,128)(2,1)} %get-tuple-element.24.refs_1_, ...), custom_call_target="tpu_custom_call" | custom-call | tf_op jit(solution)/shard_map/gather_table_0/pallas_call | solution.py:165
  55.0 0.7 fusion.4.refs_3_
  55.8 0.7 fusion.12
  56.5 0.0 copy-start.1
  56.5 1.9 %copy-done.1 = bf16[2,4,4,8,3,16,128]{6,5,4,3,2,1,0:T(8,128)(2,1)S(1)} copy-done((bf16[2,4,4,8,3,16,128]{6,5,4,3,2,1,0:T(8,128)(2,1)S(1)}, bf16[2,4,4,8,3,16,128]{6,5,4,3,2,1,0:T(8,128)(2,1)}, u32[]{:S(2)}) %copy-start.1) | copy-done | bytes 3145752
  58.4 1.6 copy-done.2
  60.0 0.9 copy-done.4
  60.9 20.2 %solve_128.1 = (f32[128,256]{1,0:T(8,128)}, bf16[6,16,128]{2,1,0:T(8,128)(2,1)S(1)}, bf16[6,16,128]{2,1,0:T(8,128)(2,1)S(1)}, bf16[4,16,128]{2,1,0:T(8,128)(2,1)S(1)}) custom-call(bf16[2,4,4,8,3,16,128]{6,5,4,3,2,1,0:T(8,128)(2,1)S(1)} %copy-done.1, bf16[2,4,4,8,3,16,128]{6,5,4,3,2,1,0:T(8,128)(2,1)} %get-tuple-element.13.refs_1_, ...), custom_call_target="tpu_custom_call" | custom-call | tf_op jit(solution)/shard_map/solve_128/pallas_call | solution.py:313
  81.1 0.6 copy-done.5
  81.7 0.6 copy-done.6
  82.3 0.6 copy-done.7
  82.9 60.2 %gather_table_1.1 = (bf16[2,4,4,8,6,16,128]{6,5,4,3,2,1,0:T(8,128)(2,1)}, bf16[2,4,4,8,6,16,128]{6,5,4,3,2,1,0:T(8,128)(2,1)}, bf16[2,8,4,4,4,16,128]{6,5,4,3,2,1,0:T(8,128)(2,1)}) custom-call(bf16[6,16,128]{2,1,0:T(8,128)(2,1)} %copy-done.5, bf16[6,16,128]{2,1,0:T(8,128)(2,1)} %copy-done.6, bf16[4,16,128]{2,1,0:T(8,128)(2,1)} %copy-done.7), custom_call_target="tpu_custom_call" | custom-call | tf_op jit(solution)/shard_map/gather_table_1/pallas_call | solution.py:165
  143.2 0.0 copy-done.8
  143.2 0.1 reshape.31
  143.3 0.0 copy-done.10
  143.3 0.1 convert_element_type.27
  143.4 0.0 copy-done.9
  143.4 0.1 reshape.32
  143.5 0.0 copy-done.3
  143.5 2.2 %copy-done = bf16[2,8,4,4,4,16,128]{6,5,4,3,2,1,0:T(8,128)(2,1)S(1)} copy-done((bf16[2,8,4,4,4,16,128]{6,5,4,3,2,1,0:T(8,128)(2,1)S(1)}, bf16[2,8,4,4,4,16,128]{6,5,4,3,2,1,0:T(8,128)(2,1)}, u32[]{:S(2)}) %copy-start) | copy-done | bytes 4194328
  145.7 23.7 %solve_64.1 = f32[64,256]{1,0:T(8,128)} custom-call(bf16[2,4,4,8,6,16,128]{6,5,4,3,2,1,0:T(8,128)(2,1)} %get-tuple-element.19.refs_0_, bf16[2,4,4,8,6,16,128]{6,5,4,3,2,1,0:T(8,128)(2,1)} %get-tuple-element.20.refs_1_, bf16[2,8,4,4,4,16,128]{6,5,4,3,2,1,0:T(8,128)(2,1)S(1)} %copy-done, s32[8,384]{1,0:T(8,128)S(1)} %fusion.10.refs_3_, ...), custom_call_target="tpu_custom_call" | custom-call | tf_op jit(solution)/shard_map/solve_64/pallas_call | solution.py:313
  (18 shorter events, 0.1 us)
Async XLA Ops:
  56.5 1.9 %copy-start.1 = (bf16[2,4,4,8,3,16,128]{6,5,4,3,2,1,0:T(8,128)(2,1)S(1)}, bf16[2,4,4,8,3,16,128]{6,5,4,3,2,1,0:T(8,128)(2,1)}, u32[]{:S(2)}) copy-start(bf16[2,4,4,8,3,16,128]{6,5,4,3,2,1,0:T(8,128)(2,1)} %get-tuple-element.12.refs_0_) | copy-start | bytes 9437188
  58.4 1.6 copy-start.2
  60.0 0.9 copy-start.4
  60.9 82.3 %copy-start.8 = (s32[64,8,6]{0,1,2:T(8,128)S(1)}, s32[64,8,6]{0,1,2:T(8,128)}, u32[]{:S(2)}) copy-start(s32[64,8,6]{0,1,2:T(8,128)} %param.13) | copy-start | bytes 36868
  60.9 82.4 %copy-start.10 = (s32[64,8,6]{0,1,2:T(8,128)S(1)}, s32[64,8,6]{0,1,2:T(8,128)}, u32[]{:S(2)}) copy-start(s32[64,8,6]{0,1,2:T(8,128)} %param.15) | copy-start | bytes 36868
  60.9 82.5 %copy-start.9 = (f32[64,8,6]{0,1,2:T(8,128)S(1)}, f32[64,8,6]{0,1,2:T(8,128)}, u32[]{:S(2)}) copy-start(f32[64,8,6]{0,1,2:T(8,128)} %param.14) | copy-start | bytes 36868
  60.9 82.6 %copy-start.3 = (f32[64,256]{1,0:T(8,128)S(1)}, f32[64,256]{1,0:T(8,128)}, u32[]{:S(2)}) copy-start(f32[64,256]{1,0:T(8,128)} %refs_6_.3) | copy-start | bytes 196612
  81.1 0.6 copy-start.5
  81.7 0.6 copy-start.6
  82.3 0.6 copy-start.7
  143.5 2.2 %copy-start = (bf16[2,8,4,4,4,16,128]{6,5,4,3,2,1,0:T(8,128)(2,1)S(1)}, bf16[2,8,4,4,4,16,128]{6,5,4,3,2,1,0:T(8,128)(2,1)}, u32[]{:S(2)}) copy-start(bf16[2,8,4,4,4,16,128]{6,5,4,3,2,1,0:T(8,128)(2,1)} %get-tuple-element.21.refs_2_) | copy-start | bytes 12582916

commit v2 on v0

v2 whole, which is shorter than its diff:
```python
import functools

import jax
import jax.numpy as jnp
from jax import lax
from jax.experimental import pallas as pl
from jax.experimental.pallas import tpu as pltpu
from jax.sharding import PartitionSpec as P

MESH = pl.DeviceIdType.MESH
CG_STEPS = 4
RANK = 256
NX, NY, NZ = 4, 4, 8
BLOCKS = 8
SIZES = {"x": NX, "y": NY, "z": NZ}
ORDERS = (("z", "y", "x"), ("z", "x", "y"), ("x", "y", "z"))
SCHEDULE = (
    (2, 0), (0, 0), (1, 0), (2, 1), (0, 1), (1, 1), (2, 0, 0), (2, 0, 1), "own", (2, 1, 0), (2, 1, 1), "z1",
    (0, 0, 0), (1, 0, 0), (2, 2, 0), (2, 2, 1), "z2", (0, 0, 1), (1, 0, 1), "beside", (2, 3, 0), "z3",
    (0, 1, 0), (1, 1, 0), "z4", "across",
)


def units_of(rows):
    units = rows // 16 * 2
    last = units // 4
    side = (units - last) // 2
    return (side, side, last)


def buffer_shape(order, units):
    return (2,) + tuple(SIZES[a] for a in order[::-1]) + (units, 16, 128)


def my_coords():
    grp, dev = lax.axis_index("grp"), lax.axis_index("dev")
    core = grp % 2
    z = grp // 2 * 2 + dev // 16
    return {"core": core, "z": z, "y": dev // 4 % 4, "x": dev % 4}


def device_at(coords):
    return {
        "grp": coords["z"] // 2 * 2 + coords["core"],
        "dev": coords["z"] % 2 * 16 + coords["y"] * 4 + coords["x"],
    }


def moved(me, axis, shift):
    size = SIZES[axis]
    return {**me, axis: (me[axis] + shift + size) % size}


def shifts_of(size):
    far = [size // 2]
    return far + [s for d in range(size // 2 - 1, 0, -1) for s in (d, -d)]


class Gather:
    def __init__(self, pieces, tables, send_sem, recv_sem, local_sem):
        self.pieces, self.tables = pieces, tables
        self.send_sem, self.recv_sem, self.local_sem = send_sem, recv_sem, local_sem
        self.me = my_coords()
        self.partner = device_at({**self.me, "core": 1 - self.me["core"]})
        self.issued, self.flying, self.handed, self.local = [], {}, {}, []

    def greet(self):
        barrier = pltpu.get_barrier_semaphore()
        others = [self.partner]
        for axis, size in SIZES.items():
            others += [device_at(moved(self.me, axis, s)) for s in shifts_of(size)]
        for other in others:
            pl.semaphore_signal(barrier, inc=1, device_id=other, device_id_type=MESH)
        pl.semaphore_wait(barrier, len(others))

    def remote(self, src, dst, target):
        e = len(self.issued)
        copy = pltpu.make_async_remote_copy(
            src_ref=src,
            dst_ref=dst,
            send_sem=self.send_sem.at[e],
            recv_sem=self.recv_sem.at[e],
            device_id=target,
            device_id_type=MESH,
        )
        copy.start()
        self.issued.append(copy)
        return copy

    def block(self, colour, phase, v, half=None):
        order, ref = ORDERS[colour], self.tables[colour]
        index = [self.me["core"]] + [self.me[order[k]] for k in range(2, phase, -1)] + [v]
        if half is not None:
            cut = ref.shape[len(index)] // 2
            index.append(pl.ds(half * cut, cut))
        return ref.at[tuple(index)]

    def send_direct(self, colour, phase):
        axis = ORDERS[colour][phase]
        dst = self.block(colour, phase, self.me[axis])
        src = self.pieces[colour] if phase == 0 else dst
        self.flying[colour, phase] = [
            self.remote(src, dst, device_at(moved(self.me, axis, s)))
            for s in shifts_of(SIZES[axis])
        ]

    def send_ring(self, colour, k, i):
        axis = ORDERS[colour][2]
        if k == SIZES[axis] // 2 - 1 and i == 1 or k == SIZES[axis] // 2:
            return
        pair = []
        for way, shift in enumerate((1, -1)):
            part = self.block(colour, 2, moved(self.me, axis, -shift * k)[axis], way ^ i)
            pair.append(self.remote(part, part, device_at(moved(self.me, axis, shift))))
        self.flying[colour, k, i] = pair

    def begin(self):
        self.greet()
        for colour in (2, 0, 1):
            self.send_direct(colour, 0)
        for colour in range(3):
            own = self.tables[colour].at[
                (self.me["core"],) + tuple(self.me[a] for a in ORDERS[colour][::-1])
            ]
            copy = pltpu.make_async_copy(self.pieces[colour], own, self.local_sem.at[colour])
            copy.start()
            self.local.append(copy)

    def take(self, token):
        colour = token[0]
        for copy in self.flying[token]:
            copy.wait_recv()
        if len(token) == 2:
            phase = token[1]
            if phase == 0:
                self.local[colour].wait()
                self.send_direct(colour, 1)
            else:
                self.send_ring(colour, 0, 0)
                self.send_ring(colour, 0, 1)
                slab = self.block(colour, 2, self.me[ORDERS[colour][2]])
                self.handed[token] = [self.remote(slab, slab, self.partner)]
            return
        k, i = token[1:]
        self.send_ring(colour, k + 1, i)
        axis = ORDERS[colour][2]
        self.handed[token] = []
        for way, shift in enumerate((1, -1)):
            got = self.block(colour, 2, moved(self.me, axis, -shift * (k + 1))[axis], way ^ i)
            self.handed[token].append(self.remote(got, got, self.partner))

    def have(self, token):
        for copy in self.handed.pop(token, ()):
            copy.wait_recv()

    def finish(self):
        for copy in self.issued:
            copy.wait_send()


def gather_copies():
    total = 0
    for order in ORDERS:
        total += SIZES[order[0]] + SIZES[order[1]] - 1
        total += 4 * (SIZES[order[2]] - 1)
    return total


def split_two(value):
    high = value.astype(jnp.bfloat16)
    low = (value - high.astype(jnp.float32)).astype(jnp.bfloat16)
    return jnp.concatenate([high, low], axis=0)


def dot(a, b):
    return jnp.dot(a, b, preferred_element_type=jnp.float32)


def groups_of(rows):
    units = units_of(rows)
    return [u // 2 for u in units], units[0] % 2


def codes_of(ids, rows):
    counts, mixed = groups_of(rows)
    owner, row = ids // rows, ids % rows
    zl, y, x = owner // 16, owner // 4 % 4, owner % 4
    group, r = row // 16, row % 16
    first = x * (128 * counts[0]) + ((zl * 4 + y) * counts[0] + group) * 16 + r
    at = 512 * counts[0]
    base = counts[0] + mixed
    second = at + y * (128 * counts[1]) + ((zl * 4 + x) * counts[1] + group - base) * 16 + r
    at += 512 * counts[1]
    base += counts[1]
    third = at + (((zl * 4 + y) * 4 + x) * counts[2] + group - base) * 16 + r
    at += 512 * counts[2]
    code = jnp.where(group < base, second, third)
    if mixed:
        shared = at + ((zl * 4 + y) * 4 + x) * 16 + r
        code = jnp.where(group == counts[0], shared, code)
    return jnp.where(group < counts[0], first, code)


def half_step_kernel(n, rows, pack, *refs):
    pieces = refs[:3]
    code_ref, weight_ref, gain_ref, start_ref = refs[3:7]
    out_ref = refs[7]
    packed = refs[8:11] if pack else ()
    scratch = refs[8 + len(packed):]
    tables = scratch[:3]
    (acc, gram, gram2, picked_t, picked, diag, gains, x_s, r_s, p_s) = scratch[3:13]
    gather = Gather(pieces, tables, *scratch[13:])
    gather.begin()

    counts, mixed = groups_of(rows)
    slots = code_ref.shape[1]
    total = slots * BLOCKS

    acc[...] = jnp.zeros_like(acc)
    gram[...] = jnp.zeros_like(gram)
    lane = lax.broadcasted_iota(jnp.int32, (n, slots), 1)
    own = lane % n == lax.broadcasted_iota(jnp.int32, (n, slots), 0)
    for g in range(BLOCKS):
        span = slice(g * slots, (g + 1) * slots)
        diag[:, span] = jnp.where(own, weight_ref[g : g + 1, :], 0.0)
        gains[:, span] = split_two(jnp.where(own, gain_ref[g : g + 1, :], 0.0))

    def add(g, parts):
        code = code_ref[pl.ds(g, 1), :]
        chosen, held = [], [[], []]
        for tiles, position in parts:
            where = lax.broadcasted_iota(jnp.int32, (16 * len(tiles), slots), 0) + position
            chosen.append(jnp.where(where == code, 1.0, 0.0).astype(jnp.bfloat16))
            for h in (0, 1):
                held[h] += [t[h] for t in tiles]
        part = jnp.concatenate([jnp.concatenate(t, axis=0) for t in held], axis=1)
        hot = jnp.concatenate(chosen, axis=0)
        product = dot(part.T, jnp.concatenate([part, hot], axis=1))
        gram[...] += product[:, 0:RANK]
        lanes = pl.ds(pl.multiple_of(g * slots, 128), slots)
        acc[:, lanes] += product[:, RANK : RANK + slots]

    me = gather.me

    def side_part(g, colour, shift):
        v = moved(me, ORDERS[colour][2], shift)[ORDERS[colour][2]]
        table, count = tables[colour], counts[colour]
        skip = mixed if colour == 1 else 0
        core, z = g % 2, g // 2 * 2
        tiles = [
            [table[core, v, a, z + zl, skip + 2 * q + h] for h in (0, 1)]
            for zl in (0, 1) for a in range(4) for q in range(count)
        ]
        return tiles, 512 * sum(counts[:colour]) + v * (128 * count)

    def shared_part(g):
        core, z = g % 2, g // 2 * 2
        tiles = [
            [tables[0][core, x, y, z + zl, 2 * counts[0]], tables[1][core, y, x, z + zl, 0]]
            for zl in (0, 1) for y in range(NY) for x in range(NX)
        ]
        return tiles, 512 * sum(counts)

    def sides(shifts, last=False):
        def block(g, _):
            parts = [side_part(g, colour, s) for colour in (0, 1) for s in shifts]
            add(g, parts + ([shared_part(g)] if last and mixed else []))
            return 0

        lax.fori_loop(0, BLOCKS, block, 0)

    def level(shift):
        v, table, count = moved(me, "z", shift)["z"], tables[2], counts[2]

        def one(core, _):
            tiles = [
                [table[core, v, y, x, 2 * q + h] for h in (0, 1)]
                for y in range(NY) for x in range(NX) for q in range(count)
            ]
            add(v // 2 * 2 + core, [(tiles, 512 * sum(counts[:2]) + v % 2 * (256 * count))])
            return 0

        lax.fori_loop(0, 2, one, 0)

    work = {
        "own": ([(0, 1), (1, 1), (2, 1)], lambda: (sides((0,)), level(0))),
        "z1": ([(2, 0, 0), (2, 0, 1)], lambda: (level(1), level(-1))),
        "z2": ([(2, 1, 0), (2, 1, 1)], lambda: (level(2), level(-2))),
        "z3": ([(2, 2, 0), (2, 2, 1)], lambda: (level(3), level(-3))),
        "z4": ([(2, 3, 0)], lambda: level(4)),
        "beside": ([(0, 0, 0), (0, 0, 1), (1, 0, 0), (1, 0, 1)], lambda: sides((1, -1))),
        "across": ([(0, 1, 0), (1, 1, 0)], lambda: sides((2,), last=True)),
    }
    for token in SCHEDULE:
        if token in work:
            needs, run = work[token]
            for need in needs:
                gather.have(need)
            run()
        else:
            gather.take(token)

    for g in range(BLOCKS):
        span = slice(g * slots, (g + 1) * slots)
        here = acc[:, span]
        picked_t[:, span] = here.astype(jnp.bfloat16)
        picked[span, :] = here.T.astype(jnp.bfloat16)
    whole = gram[...]
    high = whole.astype(jnp.bfloat16)
    gram2[:, 0:RANK] = high
    gram2[:, RANK : 2 * RANK] = (whole - high.astype(jnp.float32)).astype(jnp.bfloat16)
    width = 768

    def apply(vector):
        two = split_two(vector)
        by_gram = dot(two, gram2[...])
        image = by_gram[:n, :RANK] + by_gram[:n, RANK:] + by_gram[n:, :RANK] + vector
        extra = jnp.zeros((2 * n, RANK), jnp.float32)
        for at in range(0, total, width):
            along = dot(two, picked_t[:, at : at + width])
            along = (along[:n] + along[n:]) * diag[:, at : at + width]
            extra = extra + dot(split_two(along), picked[at : at + width, :])
        return image + extra[:n] + extra[n:]

    rhs = dot(gains[...], picked[...])
    start = start_ref[...]
    resid = rhs[:n] + rhs[n:] - apply(start)
    x_s[...] = start
    r_s[...] = resid
    p_s[...] = resid

    def step(_, now):
        direction = p_s[...]
        image = apply(direction)
        alpha = now / jnp.sum(direction * image, axis=1, keepdims=True)
        x_s[...] += alpha * direction
        left = r_s[...] - alpha * image
        r_s[...] = left
        later = jnp.sum(left * left, axis=1, keepdims=True)
        p_s[...] = left + later / now * direction
        return later

    lax.fori_loop(0, CG_STEPS, step, jnp.sum(resid * resid, axis=1, keepdims=True))
    out = x_s[...]
    out_ref[...] = out
    if pack:
        small = out.astype(jnp.bfloat16)
        many = units_of(n)
        for j in range(n // 8):
            piece = small[j // 2 * 16 : j // 2 * 16 + 16, j % 2 * 128 : j % 2 * 128 + 128]
            if j < many[0]:
                packed[0][j] = piece
            elif j < many[0] + many[1]:
                packed[1][j - many[0]] = piece
            else:
                packed[2][j - many[0] - many[1]] = piece
    gather.finish()


def half_step(pieces, codes, weights, gains, start, rows, pack):
    n, slots = start.shape[0], codes.shape[1]
    units = units_of(rows)
    total = BLOCKS * slots
    out_shape = [jax.ShapeDtypeStruct((n, RANK), jnp.float32)]
    if pack:
        out_shape += [jax.ShapeDtypeStruct((u, 16, 128), jnp.bfloat16) for u in units_of(n)]
    near = pl.BlockSpec(memory_space=pltpu.VMEM)
    copies = gather_copies()
    return pl.pallas_call(
        functools.partial(half_step_kernel, n, rows, pack),
        out_shape=out_shape,
        in_specs=[pl.BlockSpec(memory_space=pl.ANY)] * 3 + [near] * 4,
        out_specs=[near] * len(out_shape),
        scratch_shapes=[
            *(pltpu.VMEM(buffer_shape(o, u), jnp.bfloat16) for o, u in zip(ORDERS, units)),
            pltpu.VMEM((RANK, total), jnp.float32),
            pltpu.VMEM((RANK, RANK), jnp.float32),
            pltpu.VMEM((RANK, 2 * RANK), jnp.bfloat16),
            pltpu.VMEM((RANK, total), jnp.bfloat16),
            pltpu.VMEM((total, RANK), jnp.bfloat16),
            pltpu.VMEM((n, total), jnp.float32),
            pltpu.VMEM((2 * n, total), jnp.bfloat16),
            pltpu.VMEM((n, RANK), jnp.float32),
            pltpu.VMEM((n, RANK), jnp.float32),
            pltpu.VMEM((n, RANK), jnp.float32),
            pltpu.SemaphoreType.DMA((copies,)),
            pltpu.SemaphoreType.DMA((copies,)),
            pltpu.SemaphoreType.DMA((3,)),
        ],
        compiler_params=pltpu.CompilerParams(
            collective_id=0 if pack else 1, has_side_effects=True, vmem_limit_bytes=56 << 20
        ),
        name=f"half_step_{n}",
    )(*pieces, codes, weights, gains, start)


def slot_rows(array):
    n, blocks, slots = array.shape
    return array.transpose(1, 2, 0).reshape(blocks, slots * n)


def slot_inputs(slot_ids, confidence, slot_mask, rows):
    mask = slot_rows(slot_mask).astype(jnp.float32)
    conf = slot_rows(confidence)
    return codes_of(slot_rows(slot_ids), rows), mask * conf, mask * (1.0 + conf)


def per_device(
    user_factors, item_factors, user_items, user_conf, user_mask, item_users, item_conf, item_mask
):
    users, items = user_factors.shape[0], item_factors.shape[0]
    small = item_factors.astype(jnp.bfloat16).reshape(items // 16, 16, 2, 128)
    small = small.transpose(0, 2, 1, 3).reshape(items // 8, 16, 128)
    counts = units_of(items)
    pieces = jnp.split(small, [counts[0], counts[0] + counts[1]])
    inputs = slot_inputs(user_items, user_conf, user_mask, items)
    solved = half_step(pieces, *inputs, user_factors, items, True)
    inputs = slot_inputs(item_users, item_conf, item_mask, users)
    new_items = half_step(solved[1:], *inputs, item_factors, users, False)[0]
    return solved[0], new_items


def solution(mesh):
    both = ("grp", "dev")
    two, three = P(both, None), P(both, None, None)
    return jax.shard_map(
        per_device,
        mesh=mesh,
        in_specs=(two, two) + (three,) * 6,
        out_specs=(two, two),
        check_vma=False,
    )
```

time: 751 us -> 137 us (0.18)
  waiting for transfers between devices: 324 us -> 0 us
  local copies, waits for them, and re-layouts: 225 us -> 3.98 us
  Pallas kernels: 0 us -> 129 us
  matrix products: 62.8 us -> 0 us
  blocking collectives: 59.2 us -> 0 us
  other arithmetic: 58.1 us -> 3.39 us
  between operations: 15.2 us -> 0.72 us
    all_gather x2 -> x0, waiting for transfers between devices: 324 us -> none  [half_step(): whole = lax.all_gather(stacked, 'dev', axis=0, tiled=True)]
    pallas_call x0 -> x2, Pallas kernels: none -> 129 us  [half_step(): pl.pallas_call(functools.partial(half_step_kernel, n, rows, pack), out_sh...]
    gather x32 -> x0, local copies, waits for them, and re-layouts: 128 us -> none  [collect(): picked = jnp.take(whole, row_index, axis=0).astype(jnp.float32)]
    dot_general x24 -> x0, matrix products: 62.8 us -> none  [the longest x2 22.7 us: gram_of(): lax.dot_general(block, block, (((0,), (0,)), ((), ())), preferred_element...]
    all_gather x4 -> x0, blocking collectives: 59.2 us -> none  [gather_in_order(): blocks = lax.all_gather(blocks, axes[k])]
    concatenate x6 -> x0, local copies, waits for them, and re-layouts: 44.8 us -> none  [the longest x2 42.9 us: half_step(): rows = jnp.concatenate(row_parts, axis=1)]
    mul x26 -> x2, other arithmetic: 27.1 us -> 1.21 us  [slot_inputs(): mask * (1.0 + conf)]
    unnamed x9 -> x0, other arithmetic: 18 us -> none
  transfers between devices with their start and end apart: 2 -> 0, of which waited for: 2 -> 0; matrix products, arithmetic and copies ran while one was open for 2% -> 0% of each run, Pallas kernels for 0% -> 0%
where the time goes in v2:
time: 137 us
  Pallas kernels  129 us (94%)
  local copies, waits for them, and re-layouts  3.98 us (3%)
  other arithmetic  3.39 us (2%)
    pallas_call x2, Pallas kernels, half_step(): pl.pallas_call(functools.partial(half_step_kernel, n, rows, pack), out_sh...  129 us

profile of v2, /device:TPU:1, one launch (start us, length us, event | category | flops | bytes accessed | tf_op | source)
XLA Modules:
  0.0 136.9 jit_solution(18156097337891815398)
XLA Ops:
  0.6 0.8 convert_element_type.21
  1.5 0.0 copy-start.7
  1.5 0.6 fusion.22
  2.1 0.6 slice_bitcast_fusion.refs_2_
  2.7 0.0 copy-done.7
  2.7 0.1 copy-done.6
  2.8 0.6 fusion.6
  3.4 0.1 copy-done.5
  3.6 0.7 select_select_fusion.1.refs_3_
  4.2 57.1 %half_step_128.1 = (f32[128,256]{1,0:T(8,128)}, bf16[6,16,128]{2,1,0:T(8,128)(2,1)}, bf16[6,16,128]{2,1,0:T(8,128)(2,1)}, bf16[4,16,128]{2,1,0:T(8,128)(2,1)}) custom-call(bf16[3,16,128]{2,1,0:T(8,128)(2,1)} %get-tuple-element.13.refs_0_, bf16[3,16,128]{2,1,0:T(8,128)(2,1)} %get-tuple-element.12.refs_1_, bf16[2,16,128]{2,1,0:T(8,128)(2,1)} %slice_bitcast_fusion.refs_2_, ...), custom_call_target="tpu_custom_call" | custom-call | tf_op jit(solution)/shard_map/half_step_128/pallas_call | solution.py:369
  61.4 0.0 copy-start.2
  61.4 0.1 convert_element_type.27
  61.5 0.7 copy-done.2
  62.1 0.1 reshape.32
  62.2 0.6 add_multiply_fusion
  62.8 0.1 copy-done.3
  63.0 0.1 reshape.31
  63.0 0.7 select_select_fusion.refs_3_
  63.7 71.7 %half_step_64.1 = f32[64,256]{1,0:T(8,128)} custom-call(bf16[6,16,128]{2,1,0:T(8,128)(2,1)} %get-tuple-element.7.refs_0_, bf16[6,16,128]{2,1,0:T(8,128)(2,1)} %get-tuple-element.8.refs_1_, bf16[4,16,128]{2,1,0:T(8,128)(2,1)} %get-tuple-element.9.refs_2_, s32[8,384]{1,0:T(8,128)} %select_select_fusion.refs_3_, f32[8,384]{1,0:T(8,128)} %get-tuple-element.15.refs_4_, ...), custom_call_target="tpu_custom_call" | custom-call | tf_op jit(solution)/shard_map/half_step_64/pallas_call | solution.py:369
  135.4 0.0 copy-done.1
  135.4 0.0 copy-start
  135.4 0.7 copy.22
  136.1 0.2 copy-done
  136.3 0.6 copy.23
  (12 shorter events, 0.1 us)
Async XLA Ops:
  1.5 1.2 copy-start.7
  2.1 0.7 copy-start.6
  2.8 0.7 copy-start.5
  4.2 57.1 %copy-start.4 = (s32[64,8,6]{0,1,2:T(8,128)S(1)}, s32[64,8,6]{0,1,2:T(8,128)}, u32[]{:S(2)}) copy-start(s32[64,8,6]{0,1,2:T(8,128)} %param.15) | copy-start | bytes 36868
  61.4 0.7 copy-start.2
  62.2 0.7 copy-start.3
  63.0 72.4 %copy-start.1 = (f32[128,256]{1,0:T(8,128)S(1)}, f32[128,256]{1,0:T(8,128)}, u32[]{:S(2)}) copy-start(f32[128,256]{1,0:T(8,128)} %get-tuple-element.20) | copy-start | bytes 393220
  135.4 0.8 copy-start

commit v3 on v2

v3 whole, which is shorter than its diff:
```python
import functools

import jax
import jax.numpy as jnp
from jax import lax
from jax.experimental import pallas as pl
from jax.experimental.pallas import tpu as pltpu
from jax.sharding import PartitionSpec as P

MESH = pl.DeviceIdType.MESH
CG_STEPS = 4
RANK = 256
NX, NY, NZ = 4, 4, 8
BLOCKS = 8
SIZES = {"x": NX, "y": NY, "z": NZ}
ORDERS = (("z", "y", "x"), ("z", "x", "y"), ("x", "y", "z"))
SCHEDULES = {
    64: (
        ("f", 2), ("f", 0), ("s", 2, -1), ("s", 2, 1), (2, 0, 0), ("f", 1), ("s", 2, 2), ("s", 0, -1), ("s", 0, 1), (0,
        0, 0), (2, 0, -1), ("w", "z", 0), (2, 0, 1), (2, 1, 0), ("s", 1, -1), ("s", 1, 1), (2, 0, 2), ("w", "z", 1), (2,
        1, -1), ("s", 0, 2), (2, 1, 1), ("w", "z", -1), (2, 2, 0), (1, 0, 0), (2, 1, 2), ("s", 1, 2), (1, 0, -1), (0, 0,
        -1), ("w", "z", 2), (2, 2, -1), (2, 2, 1), ("w", "own", 0), (1, 0, 1), (2, 3, 0), (0, 0, 1), ("w", "own", 1),
        (2, 2, 2), ("w", "own", 2), (1, 1, 0), (0, 1, 0), (2, 3, -1), ("w", "own", 3), (2, 3, 1), (1, 0, 2), (0, 1, -1),
        (0, 0, 2), ("w", "z", -2), (1, 1, -1), (2, 3, 2), ("w", "z", 3), (0, 1, 1), ("w", "z", -3), (1, 1, 1), ("w",
        "beside", 0), ("w", "beside", 1), (1, 1, 2), (0, 1, 2), ("w", "beside", 2), ("w", "beside", 3), ("w", "z", 4)
    ),
    128: (
        ("f", 2), ("f", 0), ("s", 2, -1), ("s", 2, 1), ("f", 1), (2, 0, 0), (2, 0, -1), ("s", 0, -1), ("s", 0, 1), (0,
        0, 0), ("s", 2, 2), (2, 0, 1), ("w", "z", 0), (2, 1, 0), (2, 1, -1), ("s", 1, -1), ("s", 1, 1), (1, 0, 0), (2,
        0, 2), ("s", 0, 2), (2, 1, 1), ("w", "z", 1), (2, 2, 0), (0, 0, -1), ("w", "z", -1), (2, 2, -1), (2, 1, 2), (1,
        0, -1), (2, 2, 1), (0, 0, 1), ("w", "z", 2), (2, 3, 0), (2, 3, -1), ("w", "z", -2), (2, 2, 2), (1, 0, 1), (0, 1,
        0), (2, 3, 1), ("w", "z", 3), ("s", 1, 2), ("w", "z", -3), (1, 1, 0), (1, 1, -1), (2, 3, 2), ("w", "own", 0),
        (0, 0, 2), (0, 1, -1), ("w", "own", 1), (1, 1, 1), ("w", "own", 2), ("w", "z", 4), (0, 1, 1), (1, 0, 2), ("w",
        "own", 3), (0, 1, 2), ("w", "beside", 0), ("w", "beside", 1), (1, 1, 2), ("w", "beside", 2), ("w", "beside", 3)
    ),
}


def units_of(rows):
    units = rows // 16 * 2
    last = units // 4
    side = (units - last) // 2
    return (side, side, last)


def buffer_shape(order, units):
    return (2,) + tuple(SIZES[a] for a in order[::-1]) + (units, 16, 128)


def my_coords():
    grp, dev = lax.axis_index("grp"), lax.axis_index("dev")
    core = grp % 2
    z = grp // 2 * 2 + dev // 16
    return {"core": core, "z": z, "y": dev // 4 % 4, "x": dev % 4}


def device_at(coords):
    return {
        "grp": coords["z"] // 2 * 2 + coords["core"],
        "dev": coords["z"] % 2 * 16 + coords["y"] * 4 + coords["x"],
    }


def moved(me, axis, shift):
    size = SIZES[axis]
    return {**me, axis: (me[axis] + shift + size) % size}


def shifts_of(size):
    far = [size // 2]
    return far + [s for d in range(size // 2 - 1, 0, -1) for s in (d, -d)]


class Gather:
    def __init__(self, ring, pieces, tables, send_sem, recv_sem, local_sem):
        self.ring = ring
        self.pieces, self.tables = pieces, tables
        self.send_sem, self.recv_sem, self.local_sem = send_sem, recv_sem, local_sem
        self.me = my_coords()
        self.partner = device_at({**self.me, "core": 1 - self.me["core"]})
        self.issued, self.flying, self.handed, self.local = [], {}, {}, {}

    def greet(self):
        barrier = pltpu.get_barrier_semaphore()
        others = [self.partner]
        for axis, size in SIZES.items():
            others += [device_at(moved(self.me, axis, s)) for s in shifts_of(size)]
        for other in others:
            pl.semaphore_signal(barrier, inc=1, device_id=other, device_id_type=MESH)
        pl.semaphore_wait(barrier, len(others))

    def remote(self, src, dst, target):
        e = len(self.issued)
        copy = pltpu.make_async_remote_copy(
            src_ref=src,
            dst_ref=dst,
            send_sem=self.send_sem.at[e],
            recv_sem=self.recv_sem.at[e],
            device_id=target,
            device_id_type=MESH,
        )
        copy.start()
        self.issued.append(copy)
        return copy

    def send_first(self, colour):
        axis = ORDERS[colour][0]
        dst = self.tables[colour].at[
            (self.me["core"],) + tuple(self.me[a] for a in ORDERS[colour][::-1])
        ]
        self.flying["f", colour] = [
            self.remote(self.pieces[colour], dst, device_at(moved(self.me, axis, s)))
            for s in shifts_of(SIZES[axis])
        ]
        return dst

    def quarter(self, colour, far, s, half=None):
        _, second, last = ORDERS[colour]
        index = (self.me["core"], moved(self.me, last, far)[last], moved(self.me, second, s)[second])
        if half is not None:
            cut = self.tables[colour].shape[3] // 2
            index += (pl.ds(half * cut, cut),)
        return self.tables[colour].at[index]

    def send_second(self, colour):
        axis = ORDERS[colour][1]
        part = self.quarter(colour, 0, 0)
        for s in (1, -1) if self.ring else (1, -1, 2):
            copy = self.remote(part, part, device_at(moved(self.me, axis, s)))
            self.flying["s", colour, 2 if s == 2 else -s] = [copy]

    def send_last(self, colour, k, s):
        axis = ORDERS[colour][2]
        steps = SIZES[axis] // 2
        if k == steps:
            return
        sent = []
        for way, shift in enumerate((1, -1)):
            if k < steps - 1 or way == s % 2:
                part = self.quarter(colour, -shift * k, s)
                got = self.quarter(colour, -shift * (k + 1), s)
                sent.append((self.remote(part, part, device_at(moved(self.me, axis, shift))), got))
        self.flying[colour, k, s] = sent

    def begin(self):
        self.greet()
        for colour in (2, 0, 1):
            own = self.send_first(colour)
            copy = pltpu.make_async_copy(self.pieces[colour], own, self.local_sem.at[colour])
            copy.start()
            self.local[colour] = copy

    def take(self, token):
        if token[0] == "f":
            colour = token[1]
            for copy in self.flying[token]:
                copy.wait_recv()
            self.local[colour].wait()
            self.send_second(colour)
            self.send_last(colour, 0, 0)
        elif token[0] == "s":
            colour, s = token[1:]
            for copy in self.flying[token]:
                copy.wait_recv()
            if self.ring and s != 2:
                axis = ORDERS[colour][1]
                half = 0 if s == -1 else 1
                part = self.quarter(colour, 0, s, half)
                copy = self.remote(part, part, device_at(moved(self.me, axis, -s)))
                self.flying.setdefault(("s", colour, 2), []).append(copy)
            self.send_last(colour, 0, s)
            if s == 2:
                slab = self.tables[colour].at[self.me["core"], self.me[ORDERS[colour][2]]]
                self.handed[token] = [self.remote(slab, slab, self.partner)]
        else:
            colour, k, s = token
            arrived = self.flying[token]
            for copy, _ in arrived:
                copy.wait_recv()
            self.send_last(colour, k + 1, s)
            self.handed[token] = [self.remote(got, got, self.partner) for _, got in arrived]

    def have(self, token):
        for copy in self.handed.pop(token, ()):
            copy.wait_recv()

    def finish(self):
        for copy in self.issued:
            copy.wait_send()


def gather_copies():
    return 1 + sum(SIZES[o[0]] + SIZES[o[1]] + 1 + 12 * (SIZES[o[2]] - 2) for o in ORDERS)


def split_two(value):
    high = value.astype(jnp.bfloat16)
    low = (value - high.astype(jnp.float32)).astype(jnp.bfloat16)
    return jnp.concatenate([high, low], axis=0)


def dot(a, b):
    return jnp.dot(a, b, preferred_element_type=jnp.float32)


def groups_of(rows):
    units = units_of(rows)
    return [u // 2 for u in units], units[0] % 2


def codes_of(ids, rows):
    counts, mixed = groups_of(rows)
    bits = rows.bit_length() - 1
    owner, row = ids >> bits, ids & (rows - 1)
    zl, y, x = owner >> 4, (owner >> 2) & 3, owner & 3
    group, r = row >> 4, row & 15
    first = x * (128 * counts[0]) + ((zl * 4 + y) * counts[0] + group) * 16 + r
    at = 512 * counts[0]
    base = counts[0] + mixed
    second = at + y * (128 * counts[1]) + ((zl * 4 + x) * counts[1] + group - base) * 16 + r
    at += 512 * counts[1]
    base += counts[1]
    third = at + (((zl * 4 + y) * 4 + x) * counts[2] + group - base) * 16 + r
    at += 512 * counts[2]
    code = jnp.where(group < base, second, third)
    if mixed:
        shared = at + ((zl * 4 + y) * 4 + x) * 16 + r
        code = jnp.where(group == counts[0], shared, code)
    return jnp.where(group < counts[0], first, code)


def half_step_kernel(n, rows, pack, *refs):
    pieces_ref, ids_ref, conf_ref, mask_ref, start_ref, out_ref = refs[:6]
    packed = refs[6] if pack else None
    scratch = refs[7:] if pack else refs[6:]
    pieces, at = [], 0
    for u in units_of(rows):
        pieces.append(pieces_ref.at[pl.ds(at, u)])
        at += u
    tables = scratch[:3]
    (acc, gram, other, gram2, picked_t, picked, diag, gains, columns, x_s, r_s, p_s) = scratch[3:15]
    gather = Gather(not pack, pieces, tables, *scratch[15:])
    gather.begin()

    counts, mixed = groups_of(rows)
    slots = n * ids_ref.shape[0]

    def along_lanes(ref):
        return jnp.concatenate([ref[k] for k in range(ref.shape[0])], axis=1)

    code = codes_of(along_lanes(ids_ref), rows)
    mask = along_lanes(mask_ref).astype(jnp.float32)
    conf = along_lanes(conf_ref)
    weight, gain = mask * conf, mask * (1.0 + conf)
    total = slots * BLOCKS

    acc[...] = jnp.zeros_like(acc)
    gram[...] = jnp.zeros_like(gram)
    lane = lax.broadcasted_iota(jnp.int32, (n, slots), 1)
    own = lane % n == lax.broadcasted_iota(jnp.int32, (n, slots), 0)
    for g in range(BLOCKS):
        span = slice(g * slots, (g + 1) * slots)
        diag[:, span] = jnp.where(own, weight[g : g + 1, :], 0.0)
        gains[:, span] = split_two(jnp.where(own, gain[g : g + 1, :], 0.0))
        for at in range(0, slots, 128):
            row = jnp.broadcast_to(code[g : g + 1, at : at + 128], (128, 128))
            columns[pl.ds(g * slots + at, 128), :] = row.T

    def add(g, parts, with_gram):
        at = pl.ds(pl.multiple_of(g * slots, 128), slots)
        code = columns[at, :]
        lane = lax.broadcasted_iota(jnp.int32, (slots, 128), 1)
        chosen, held = [], [[], []]
        for tiles, position in parts:
            for first in range(0, 16 * len(tiles), 128):
                hit = lane + (position + first) == code
                chosen.append(jnp.where(hit, 1.0, 0.0).astype(jnp.bfloat16))
            for h in (0, 1):
                held[h] += [t[h] for t in tiles]
        part = jnp.concatenate([jnp.concatenate(t, axis=0) for t in held], axis=1)
        if with_gram:
            gram[...] += dot(part.T, part)
        acc[at, :] += dot(jnp.concatenate(chosen, axis=1), part)

    me = gather.me

    def side_part(g, colour, shift):
        v = moved(me, ORDERS[colour][2], shift)[ORDERS[colour][2]]
        table, count = tables[colour], counts[colour]
        skip = mixed if colour == 1 else 0
        core, z = g % 2, g // 2 * 2
        tiles = [
            [table[core, v, a, z + zl, skip + 2 * q + h] for h in (0, 1)]
            for zl in (0, 1) for a in range(4) for q in range(count)
        ]
        return tiles, 512 * sum(counts[:colour]) + v * (128 * count)

    def shared_part(g):
        core, z = g % 2, g // 2 * 2
        tiles = [
            [tables[0][core, x, y, z + zl, 2 * counts[0]], tables[1][core, y, x, z + zl, 0]]
            for zl in (0, 1) for y in range(NY) for x in range(NX)
        ]
        return tiles, 512 * sum(counts)

    def sides(shifts, pair, last=False):
        for mine in (True, False):
            g = 2 * pair + (me["core"] if mine else 1 - me["core"])
            parts = [side_part(g, colour, s) for colour in (0, 1) for s in shifts]
            add(g, parts + ([shared_part(g)] if last and mixed else []), mine)

    def level(shift):
        v, table, count = moved(me, "z", shift)["z"], tables[2], counts[2]
        for mine in (True, False):
            core = me["core"] if mine else 1 - me["core"]
            tiles = [
                [table[core, v, y, x, 2 * q + h] for h in (0, 1)]
                for y in range(NY) for x in range(NX) for q in range(count)
            ]
            position = 512 * sum(counts[:2]) + v % 2 * (256 * count)
            add(v // 2 * 2 + core, [(tiles, position)], mine)

    def across(pair, _):
        sides((2,), pair, last=True)
        return 0

    def work(what, which):
        every = (0, 1, -1, 2)
        if what == "own":
            needs, run = [("s", c, 2) for c in (0, 1)], lambda: sides((0,), which)
        elif what == "beside":
            needs = [(c, 0, s) for c in (0, 1) for s in every]
            run = lambda: sides((1, -1), which)
        elif what == "across":
            needs, run = [(c, 1, s) for c in (0, 1) for s in every], lambda: lax.fori_loop(0, BLOCKS // 2, across, 0)
        else:
            needs = [(2, abs(which) - 1, s) for s in every] if which else [("s", 2, 2)]
            run = lambda: level(which)
        for need in needs:
            gather.have(need)
        run()

    for token in SCHEDULES[rows] + (("w", "across", 0),):
        if token[0] == "w":
            work(*token[1:])
        else:
            gather.take(token)

    for g in range(BLOCKS):
        span = slice(g * slots, (g + 1) * slots)
        here = acc[span, :]
        picked[span, :] = here.astype(jnp.bfloat16)
        picked_t[:, span] = here.T.astype(jnp.bfloat16)
        if g == 1:
            swap = gather.remote(gram, other, gather.partner)
    rhs = dot(gains[...], picked[...])
    swap.wait_recv()
    whole = gram[...] + other[...]
    high = whole.astype(jnp.bfloat16)
    gram2[:, 0:RANK] = high
    gram2[:, RANK : 2 * RANK] = (whole - high.astype(jnp.float32)).astype(jnp.bfloat16)
    width = 768

    def apply(vector):
        two = split_two(vector)
        by_gram = dot(two, gram2[...])
        image = by_gram[:n, :RANK] + by_gram[:n, RANK:] + by_gram[n:, :RANK] + vector
        extra = jnp.zeros((2 * n, RANK), jnp.float32)
        for at in range(0, total, width):
            along = dot(two, picked_t[:, at : at + width])
            along = (along[:n] + along[n:]) * diag[:, at : at + width]
            extra = extra + dot(split_two(along), picked[at : at + width, :])
        return image + extra[:n] + extra[n:]

    start = start_ref[...]
    resid = rhs[:n] + rhs[n:] - apply(start)
    x_s[...] = start
    r_s[...] = resid
    p_s[...] = resid

    def step(_, now):
        direction = p_s[...]
        image = apply(direction)
        alpha = now / jnp.sum(direction * image, axis=1, keepdims=True)
        x_s[...] += alpha * direction
        left = r_s[...] - alpha * image
        r_s[...] = left
        later = jnp.sum(left * left, axis=1, keepdims=True)
        p_s[...] = left + later / now * direction
        return later

    lax.fori_loop(0, CG_STEPS, step, jnp.sum(resid * resid, axis=1, keepdims=True))
    out = x_s[...]
    out_ref[...] = out
    if pack:
        small = out.astype(jnp.bfloat16)
        for j in range(n // 8):
            packed[j] = small[j // 2 * 16 : j // 2 * 16 + 16, j % 2 * 128 : j % 2 * 128 + 128]
    gather.finish()


def half_step(pieces, slot_arrays, start, rows, pack):
    n, slots = start.shape[0], start.shape[0] * slot_arrays[0].shape[2]
    units = units_of(rows)
    total = BLOCKS * slots
    out_shape = [jax.ShapeDtypeStruct((n, RANK), jnp.float32)]
    if pack:
        out_shape.append(jax.ShapeDtypeStruct((n // 8, 16, 128), jnp.bfloat16))
    near = pl.BlockSpec(memory_space=pltpu.VMEM)
    copies = gather_copies()
    return pl.pallas_call(
        functools.partial(half_step_kernel, n, rows, pack),
        out_shape=out_shape,
        in_specs=[pl.BlockSpec(memory_space=pl.ANY)] + [near] * 4,
        out_specs=[near] * len(out_shape),
        scratch_shapes=[
            *(pltpu.VMEM(buffer_shape(o, u), jnp.bfloat16) for o, u in zip(ORDERS, units)),
            pltpu.VMEM((total, RANK), jnp.float32),
            pltpu.VMEM((RANK, RANK), jnp.float32),
            pltpu.VMEM((RANK, RANK), jnp.float32),
            pltpu.VMEM((RANK, 2 * RANK), jnp.bfloat16),
            pltpu.VMEM((RANK, total), jnp.bfloat16),
            pltpu.VMEM((total, RANK), jnp.bfloat16),
            pltpu.VMEM((n, total), jnp.float32),
            pltpu.VMEM((2 * n, total), jnp.bfloat16),
            pltpu.VMEM((total, 128), jnp.int32),
            pltpu.VMEM((n, RANK), jnp.float32),
            pltpu.VMEM((n, RANK), jnp.float32),
            pltpu.VMEM((n, RANK), jnp.float32),
            pltpu.SemaphoreType.DMA((copies,)),
            pltpu.SemaphoreType.DMA((copies,)),
            pltpu.SemaphoreType.DMA((3,)),
        ],
        compiler_params=pltpu.CompilerParams(
            collective_id=0 if pack else 1, has_side_effects=True, vmem_limit_bytes=60 << 20
        ),
        name=f"half_step_{n}",
    )(pieces, *(a.transpose(2, 1, 0) for a in slot_arrays), start)


def per_device(
    user_factors, item_factors, user_items, user_conf, user_mask, item_users, item_conf, item_mask
):
    users, items = user_factors.shape[0], item_factors.shape[0]
    small = item_factors.astype(jnp.bfloat16).reshape(items // 16, 16, 2, 128)
    small = small.transpose(0, 2, 1, 3).reshape(items // 8, 16, 128)
    new_users, pieces = half_step(small, (user_items, user_conf, user_mask), user_factors, items, True)
    new_items = half_step(pieces, (item_users, item_conf, item_mask), item_factors, users, False)[0]
    return new_users, new_items


def solution(mesh):
    both = ("grp", "dev")
    two, three = P(both, None), P(both, None, None)
    return jax.shard_map(
        per_device,
        mesh=mesh,
        in_specs=(two, two) + (three,) * 6,
        out_specs=(two, two),
        check_vma=False,
    )
```

time: 137 us -> 126 us (0.920)
  Pallas kernels: 129 us -> 123 us
  other arithmetic: 3.39 us -> 0.85 us
  local copies, waits for them, and re-layouts: 3.98 us -> 2.11 us
    pallas_call x2, Pallas kernels: 129 us -> 123 us  [half_step(): pl.pallas_call(functools.partial(half_step_kernel, n, rows, pack), out_sh...]
where the time goes in v3:
time: 126 us
  Pallas kernels  123 us (98%)
  local copies, waits for them, and re-layouts  2.11 us (2%)
    pallas_call x2, Pallas kernels, half_step(): pl.pallas_call(functools.partial(half_step_kernel, n, rows, pack), out_sh...  123 us

profile of v3, /device:TPU:1, one launch (start us, length us, event | category | flops | bytes accessed | tf_op | source)
XLA Modules:
  0.0 126.1 jit_solution(7313727246959278115)
XLA Ops:
  0.6 0.8 convert_element_type.3
  1.5 0.6 copy.10
  2.1 56.7 %half_step_128.1 = (f32[128,256]{1,0:T(8,128)}, bf16[16,16,128]{2,1,0:T(8,128)(2,1)}) custom-call(bf16[8,16,128]{2,1,0:T(8,128)(2,1)} %bitcast.9, s32[3,8,128]{2,1,0:T(8,128)} %bitcast.13, f32[3,8,128]{2,1,0:T(8,128)} %bitcast.14, s32[3,8,128]{2,1,0:T(8,128)} %bitcast.15, f32[128,256]{1,0:T(8,128)} %refs_4_.2), custom_call_target="tpu_custom_call" | custom-call | tf_op jit(solution)/shard_map/half_step_128/pallas_call | solution.py:411
  58.8 0.0 copy-start.1
  58.9 65.8 %half_step_64.1 = f32[64,256]{1,0:T(8,128)} custom-call(bf16[16,16,128]{2,1,0:T(8,128)(2,1)} %get-tuple-element.5.refs_0_, s32[6,8,64]{2,1,0:T(8,128)} %bitcast.10, f32[6,8,64]{2,1,0:T(8,128)} %bitcast.11, s32[6,8,64]{2,1,0:T(8,128)} %bitcast.12, f32[64,256]{1,0:T(8,128)} %refs_4_.3), custom_call_target="tpu_custom_call" | custom-call | tf_op jit(solution)/shard_map/half_step_64/pallas_call | solution.py:411
  124.7 0.0 copy-done.1
  124.7 0.0 copy-start
  124.7 0.7 copy.13
  125.3 0.2 copy-done
  125.5 0.6 copy.14
  (1 shorter events, 0.0 us)
Async XLA Ops:
  58.8 65.8 %copy-start.1 = (f32[128,256]{1,0:T(8,128)S(1)}, f32[128,256]{1,0:T(8,128)}, u32[]{:S(2)}) copy-start(f32[128,256]{1,0:T(8,128)} %get-tuple-element.8) | copy-start | bytes 393220
  124.7 0.8 copy-start

commit v4 on v3

--- a/solution.py
+++ b/solution.py
@@ -13,25 +13,29 @@
 NX, NY, NZ = 4, 4, 8
 BLOCKS = 8
 SIZES = {"x": NX, "y": NY, "z": NZ}
-ORDERS = (("z", "y", "x"), ("z", "x", "y"), ("x", "y", "z"))
+ORDERS = (("y", "z", "x"), ("z", "x", "y"), ("x", "y", "z"))
 SCHEDULES = {
     64: (
-        ("f", 2), ("f", 0), ("s", 2, -1), ("s", 2, 1), (2, 0, 0), ("f", 1), ("s", 2, 2), ("s", 0, -1), ("s", 0, 1), (0,
-        0, 0), (2, 0, -1), ("w", "z", 0), (2, 0, 1), (2, 1, 0), ("s", 1, -1), ("s", 1, 1), (2, 0, 2), ("w", "z", 1), (2,
-        1, -1), ("s", 0, 2), (2, 1, 1), ("w", "z", -1), (2, 2, 0), (1, 0, 0), (2, 1, 2), ("s", 1, 2), (1, 0, -1), (0, 0,
-        -1), ("w", "z", 2), (2, 2, -1), (2, 2, 1), ("w", "own", 0), (1, 0, 1), (2, 3, 0), (0, 0, 1), ("w", "own", 1),
-        (2, 2, 2), ("w", "own", 2), (1, 1, 0), (0, 1, 0), (2, 3, -1), ("w", "own", 3), (2, 3, 1), (1, 0, 2), (0, 1, -1),
-        (0, 0, 2), ("w", "z", -2), (1, 1, -1), (2, 3, 2), ("w", "z", 3), (0, 1, 1), ("w", "z", -3), (1, 1, 1), ("w",
-        "beside", 0), ("w", "beside", 1), (1, 1, 2), (0, 1, 2), ("w", "beside", 2), ("w", "beside", 3), ("w", "z", 4)
+        ("f", 2), ("f", 0), ("f", 1), ("s", 2, -1), ("s", 2, 1), (2, 0, 0), (0, 0, 0), ("s", 0, -1), ("s", 0, 1), ("s",
+        2, 2), ("w", "z", 0), ("s", 1, -1), ("s", 1, 1), (1, 0, 0), (2, 0, -1), (2, 0, 1), (2, 1, 0), ("s", 0, -2),
+        ("s", 0, 2), (2, 0, 2), (2, 1, -1), ("s", 1, 2), (0, 1, 0), ("w", "z", 1), (2, 1, 1), (1, 0, -1), (2, 2, 0), (0,
+        0, -1), ("w", "z", -1), (0, 0, 1), ("s", 0, -3), ("s", 0, 3), (1, 0, 1), (2, 1, 2), (0, 0, -2), (2, 2, -1), (0,
+        0, 2), ("w", "z", 2), (2, 2, 1), (1, 1, 0), (2, 3, 0), ("w", "z", -2), (0, 1, -1), ("s", 0, 4), (1, 0, 2), (0,
+        1, 1), (2, 2, 2), (1, 1, -1), (0, 0, -3), ("w", "own", 0), (2, 3, -1), (0, 0, 3), (2, 3, 1), (0, 1, -2), ("w",
+        "own", 1), (1, 1, 1), (0, 1, 2), ("w", "own", 2), ("w", "own", 3), (0, 0, 4), (2, 3, 2), ("w", "z", 3), (1, 1,
+        2), (0, 1, -3), ("w", "z", -3), (0, 1, 3), ("w", "beside", 0), ("w", "beside", 1), (0, 1, 4), ("w", "beside",
+        2), ("w", "beside", 3), ("w", "z", 4)
     ),
     128: (
-        ("f", 2), ("f", 0), ("s", 2, -1), ("s", 2, 1), ("f", 1), (2, 0, 0), (2, 0, -1), ("s", 0, -1), ("s", 0, 1), (0,
-        0, 0), ("s", 2, 2), (2, 0, 1), ("w", "z", 0), (2, 1, 0), (2, 1, -1), ("s", 1, -1), ("s", 1, 1), (1, 0, 0), (2,
-        0, 2), ("s", 0, 2), (2, 1, 1), ("w", "z", 1), (2, 2, 0), (0, 0, -1), ("w", "z", -1), (2, 2, -1), (2, 1, 2), (1,
-        0, -1), (2, 2, 1), (0, 0, 1), ("w", "z", 2), (2, 3, 0), (2, 3, -1), ("w", "z", -2), (2, 2, 2), (1, 0, 1), (0, 1,
-        0), (2, 3, 1), ("w", "z", 3), ("s", 1, 2), ("w", "z", -3), (1, 1, 0), (1, 1, -1), (2, 3, 2), ("w", "own", 0),
-        (0, 0, 2), (0, 1, -1), ("w", "own", 1), (1, 1, 1), ("w", "own", 2), ("w", "z", 4), (0, 1, 1), (1, 0, 2), ("w",
-        "own", 3), (0, 1, 2), ("w", "beside", 0), ("w", "beside", 1), (1, 1, 2), ("w", "beside", 2), ("w", "beside", 3)
+        ("f", 2), ("f", 0), ("f", 1), ("s", 2, -1), ("s", 2, 1), (2, 0, 0), (0, 0, 0), ("s", 0, -1), ("s", 0, 1), (2, 0,
+        -1), (2, 0, 1), ("s", 1, -1), ("s", 1, 1), (1, 0, 0), ("s", 2, 2), (2, 1, 0), (0, 1, 0), ("w", "z", 0), ("s", 0,
+        -2), ("s", 0, 2), (0, 0, -1), (2, 1, -1), (2, 1, 1), (0, 0, 1), (2, 0, 2), (1, 0, -1), ("s", 1, 2), (2, 2, 0),
+        ("w", "z", 1), ("w", "z", -1), (0, 0, -2), ("s", 0, -3), ("s", 0, 3), (1, 0, 1), (2, 2, -1), (0, 0, 2), (0, 1,
+        -1), (2, 2, 1), (2, 1, 2), (0, 1, 1), (1, 1, 0), (1, 1, -1), (0, 1, -2), (2, 3, 0), ("w", "z", 2), ("s", 0, 4),
+        (2, 3, -1), ("w", "z", -2), (0, 0, -3), (2, 3, 1), ("w", "own", 0), (2, 2, 2), (1, 0, 2), (0, 0, 3), ("w",
+        "own", 1), (0, 1, 2), ("w", "own", 2), ("w", "z", 3), (1, 1, 1), (0, 0, 4), (2, 3, 2), (0, 1, -3), ("w", "own",
+        3), ("w", "z", -3), (0, 1, 3), (1, 1, 2), ("w", "beside", 0), (0, 1, 4), ("w", "beside", 1), ("w", "beside", 2),
+        ("w", "beside", 3), ("w", "z", 4)
     ),
 }
 
@@ -64,6 +68,11 @@
 def moved(me, axis, shift):
     size = SIZES[axis]
     return {**me, axis: (me[axis] + shift + size) % size}
+
+
+def parts_of(colour):
+    size = SIZES[ORDERS[colour][1]]
+    return (0,) + tuple(shifts_of(size))
 
 
 def shifts_of(size):
@@ -122,10 +131,13 @@
             index += (pl.ds(half * cut, cut),)
         return self.tables[colour].at[index]
 
+    def rings(self, colour):
+        return self.ring or SIZES[ORDERS[colour][1]] > 4
+
     def send_second(self, colour):
         axis = ORDERS[colour][1]
         part = self.quarter(colour, 0, 0)
-        for s in (1, -1) if self.ring else (1, -1, 2):
+        for s in (1, -1) if self.rings(colour) else (1, -1, 2):
             copy = self.remote(part, part, device_at(moved(self.me, axis, s)))
             self.flying["s", colour, 2 if s == 2 else -s] = [copy]
 
@@ -162,14 +174,16 @@
             colour, s = token[1:]
             for copy in self.flying[token]:
                 copy.wait_recv()
-            if self.ring and s != 2:
-                axis = ORDERS[colour][1]
-                half = 0 if s == -1 else 1
+            axis = ORDERS[colour][1]
+            far, way = SIZES[axis] // 2, 1 if s > 0 else -1
+            if self.rings(colour) and s != far:
+                half = None if abs(s) < far - 1 else 0 if s < 0 else 1
                 part = self.quarter(colour, 0, s, half)
-                copy = self.remote(part, part, device_at(moved(self.me, axis, -s)))
-                self.flying.setdefault(("s", colour, 2), []).append(copy)
+                copy = self.remote(part, part, device_at(moved(self.me, axis, -way)))
+                key = ("s", colour, far if half is not None else s + way)
+                self.flying.setdefault(key, []).append(copy)
             self.send_last(colour, 0, s)
-            if s == 2:
+            if s == far:
                 slab = self.tables[colour].at[self.me["core"], self.me[ORDERS[colour][2]]]
                 self.handed[token] = [self.remote(slab, slab, self.partner)]
         else:
@@ -190,7 +204,10 @@
 
 
 def gather_copies():
-    return 1 + sum(SIZES[o[0]] + SIZES[o[1]] + 1 + 12 * (SIZES[o[2]] - 2) for o in ORDERS)
+    total = 1
+    for first, second, last in ORDERS:
+        total += SIZES[first] + SIZES[second] + 2 * SIZES[second] * (SIZES[last] - 1)
+    return total
 
 
 def split_two(value):
@@ -290,7 +307,7 @@
         skip = mixed if colour == 1 else 0
         core, z = g % 2, g // 2 * 2
         tiles = [
-            [table[core, v, a, z + zl, skip + 2 * q + h] for h in (0, 1)]
+            [table[(core, v) + ((a, z + zl) if colour else (z + zl, a)) + (skip + 2 * q + h,)] for h in (0, 1)]
             for zl in (0, 1) for a in range(4) for q in range(count)
         ]
         return tiles, 512 * sum(counts[:colour]) + v * (128 * count)
@@ -298,7 +315,7 @@
     def shared_part(g):
         core, z = g % 2, g // 2 * 2
         tiles = [
-            [tables[0][core, x, y, z + zl, 2 * counts[0]], tables[1][core, y, x, z + zl, 0]]
+            [tables[0][core, x, z + zl, y, 2 * counts[0]], tables[1][core, y, x, z + zl, 0]]
             for zl in (0, 1) for y in range(NY) for x in range(NX)
         ]
         return tiles, 512 * sum(counts)
@@ -325,16 +342,17 @@
         return 0
 
     def work(what, which):
-        every = (0, 1, -1, 2)
+        last = [parts_of(c)[1] for c in range(3)]
         if what == "own":
-            needs, run = [("s", c, 2) for c in (0, 1)], lambda: sides((0,), which)
+            needs, run = [("s", c, last[c]) for c in (0, 1)], lambda: sides((0,), which)
         elif what == "beside":
-            needs = [(c, 0, s) for c in (0, 1) for s in every]
+            needs = [(c, 0, s) for c in (0, 1) for s in parts_of(c)]
             run = lambda: sides((1, -1), which)
         elif what == "across":
-            needs, run = [(c, 1, s) for c in (0, 1) for s in every], lambda: lax.fori_loop(0, BLOCKS // 2, across, 0)
+            needs = [(c, 1, s) for c in (0, 1) for s in parts_of(c)]
+            run = lambda: lax.fori_loop(0, BLOCKS // 2, across, 0)
         else:
-            needs = [(2, abs(which) - 1, s) for s in every] if which else [("s", 2, 2)]
+            needs = [(2, abs(which) - 1, s) for s in parts_of(2)] if which else [("s", 2, last[2])]
             run = lambda: level(which)
         for need in needs:
             gather.have(need)

time: 126 us -> 123 us (0.976)
  Pallas kernels: 123 us -> 119 us
    pallas_call x2, Pallas kernels: 123 us -> 119 us  [half_step(): pl.pallas_call(functools.partial(half_step_kernel, n, rows, pack), out_sh...]
where the time goes in v4:
time: 123 us
  Pallas kernels  119 us (97%)
  local copies, waits for them, and re-layouts  2.11 us (2%)
    pallas_call x2, Pallas kernels, half_step(): pl.pallas_call(functools.partial(half_step_kernel, n, rows, pack), out_sh...  119 us

profile of v4, /device:TPU:1, one launch (start us, length us, event | category | flops | bytes accessed | tf_op | source)
XLA Modules:
  0.0 122.8 jit_solution(862262456973910037)
XLA Ops:
  0.6 0.8 convert_element_type.3
  1.5 0.6 copy.10
  2.1 57.5 %half_step_128.1 = (f32[128,256]{1,0:T(8,128)}, bf16[16,16,128]{2,1,0:T(8,128)(2,1)}) custom-call(bf16[8,16,128]{2,1,0:T(8,128)(2,1)} %bitcast.9, s32[3,8,128]{2,1,0:T(8,128)} %bitcast.13, f32[3,8,128]{2,1,0:T(8,128)} %bitcast.14, s32[3,8,128]{2,1,0:T(8,128)} %bitcast.15, f32[128,256]{1,0:T(8,128)} %refs_4_.2), custom_call_target="tpu_custom_call" | custom-call | tf_op jit(solution)/shard_map/half_step_128/pallas_call | solution.py:429
  59.6 0.0 copy-start.1
  59.7 61.6 %half_step_64.1 = f32[64,256]{1,0:T(8,128)} custom-call(bf16[16,16,128]{2,1,0:T(8,128)(2,1)} %get-tuple-element.5.refs_0_, s32[6,8,64]{2,1,0:T(8,128)} %bitcast.10, f32[6,8,64]{2,1,0:T(8,128)} %bitcast.11, s32[6,8,64]{2,1,0:T(8,128)} %bitcast.12, f32[64,256]{1,0:T(8,128)} %refs_4_.3), custom_call_target="tpu_custom_call" | custom-call | tf_op jit(solution)/shard_map/half_step_64/pallas_call | solution.py:429
  121.3 0.0 copy-done.1
  121.3 0.0 copy-start
  121.3 0.7 copy.13
  121.9 0.2 copy-done
  122.1 0.6 copy.14
  (1 shorter events, 0.0 us)
Async XLA Ops:
  59.6 61.6 %copy-start.1 = (f32[128,256]{1,0:T(8,128)S(1)}, f32[128,256]{1,0:T(8,128)}, u32[]{:S(2)}) copy-start(f32[128,256]{1,0:T(8,128)} %get-tuple-element.8) | copy-start | bytes 393220
  121.3 0.8 copy-start

commit v5 on v4

--- a/solution.py
+++ b/solution.py
@@ -366,9 +366,9 @@
 
     for g in range(BLOCKS):
         span = slice(g * slots, (g + 1) * slots)
-        here = acc[span, :]
-        picked[span, :] = here.astype(jnp.bfloat16)
-        picked_t[:, span] = here.T.astype(jnp.bfloat16)
+        here = acc[span, :].astype(jnp.bfloat16)
+        picked[span, :] = here
+        picked_t[:, span] = here.T
         if g == 1:
             swap = gather.remote(gram, other, gather.partner)
     rhs = dot(gains[...], picked[...])

time: 123 us -> 123 us (level)
  no operation moved by 1% of the time
where the time goes in v5:
time: 123 us
  Pallas kernels  119 us (97%)
  local copies, waits for them, and re-layouts  2.11 us (2%)
    pallas_call x2, Pallas kernels, half_step(): pl.pallas_call(functools.partial(half_step_kernel, n, rows, pack), out_sh...  119 us

profile of v5, /device:TPU:1, one launch (start us, length us, event | category | flops | bytes accessed | tf_op | source)
XLA Modules:
  0.0 122.7 jit_solution(9430805826821293246)
XLA Ops:
  0.6 0.8 convert_element_type.3
  1.5 0.6 copy.10
  2.1 57.5 %half_step_128.1 = (f32[128,256]{1,0:T(8,128)}, bf16[16,16,128]{2,1,0:T(8,128)(2,1)}) custom-call(bf16[8,16,128]{2,1,0:T(8,128)(2,1)} %bitcast.9, s32[3,8,128]{2,1,0:T(8,128)} %bitcast.13, f32[3,8,128]{2,1,0:T(8,128)} %bitcast.14, s32[3,8,128]{2,1,0:T(8,128)} %bitcast.15, f32[128,256]{1,0:T(8,128)} %refs_4_.2), custom_call_target="tpu_custom_call" | custom-call | tf_op jit(solution)/shard_map/half_step_128/pallas_call | solution.py:429
  59.6 0.0 copy-start.1
  59.6 61.6 %half_step_64.1 = f32[64,256]{1,0:T(8,128)} custom-call(bf16[16,16,128]{2,1,0:T(8,128)(2,1)} %get-tuple-element.5.refs_0_, s32[6,8,64]{2,1,0:T(8,128)} %bitcast.10, f32[6,8,64]{2,1,0:T(8,128)} %bitcast.11, s32[6,8,64]{2,1,0:T(8,128)} %bitcast.12, f32[64,256]{1,0:T(8,128)} %refs_4_.3), custom_call_target="tpu_custom_call" | custom-call | tf_op jit(solution)/shard_map/half_step_64/pallas_call | solution.py:429
  121.2 0.0 copy-done.1
  121.3 0.0 copy-start
  121.3 0.7 copy.13
  121.9 0.2 copy-done
  122.1 0.6 copy.14
  (1 shorter events, 0.0 us)
Async XLA Ops:
  59.6 61.6 %copy-start.1 = (f32[128,256]{1,0:T(8,128)S(1)}, f32[128,256]{1,0:T(8,128)}, u32[]{:S(2)}) copy-start(f32[128,256]{1,0:T(8,128)} %get-tuple-element.8) | copy-start | bytes 393220
  121.3 0.8 copy-start
